TPU v7x, 128 devices: a whole 4x4x4 slice. The times are simulated.
128 devices in a mesh: lat: 8 (over x_hi, y), grp: 16 (over z, x_lo, core).
Axes of the slice: x: 4 (x_hi: 2, x_lo: 2; x = x_hi * 2 + x_lo), y: 4, z: 4, core: 2. Of those that a mesh axis runs over, the one named last changes fastest.
Arguments:
- fields: float32 [512, 30, 64, 128], P('grp', None, 'lat'), may hold values from -6 to 6
- diffusion: float32 [64, 128], P('lat'), may hold values from 0.12 to 0.245
- mixing: float32 [30, 30], replicated, may hold values from -0.08 to 1
- heating: float32 [30, 64, 128], P(None, 'lat'), may hold values from -2 to 2
- land_mask: int32 [64, 128], P('lat'), may hold values 0 or 1
- conv_weight: float32 [32, 27], replicated, may hold values from -1.25 to 1.25
- head_weight: float32 [32, 64, 128], P(None, 'lat'), may hold values from -0.01171875 to 0.01171875
- counts: int32 [512], replicated, may hold values from 0 to 32, as said below
- source: int32 [512], replicated, may hold values from 0 to 511, as said below
Outputs:
- new_fields: float32 [512, 30, 64, 128], P('grp', None, 'lat')
- scores: float32 [512], P('grp')
- slot_weight: float32 [512], P('grp')
Inputs may be any that keep to these rules, and one draw needn't show every extreme that they name: Members 32 g to 32 g + 31 form group g. In every group exactly one member has a count of 2 or more and every group has a member of count 0; the counts sum to 512. source[s] = s where the member s has a count of 1 or more. Every slot s of count 0 takes the member of count 2 or more of one other group, the same group for all such slots of s's group, each group's such member is taken by the slots of exactly one other group, and a member of count c is taken by c - 1 slots.
All inputs are finite; a program needn't handle non-finite values. No bound on the sum of `land_mask` on one device may be relied on, other than what follows from the above.
Results may differ from a plain program's by a relative error of at most 0.0003.
Values sent between devices are 32-bit elements; how exact they have to be, the bound alone decides.
No kernel may reach another device: no remote copies, remote signals or barrier semaphores. Data moves between devices by JAX's collectives and lax.ppermute only.
A program may use at most 128 MiB of HBM per device.

v0:
```python
import functools

import jax
import jax.numpy as jnp
import numpy as np
from jax import lax
from jax.experimental import pallas as pl
from jax.experimental.pallas import tpu as pltpu
from jax.sharding import PartitionSpec as P


LEV = 10
STEPS = 4
STARTS = (0, 8, 16, 22)
DEEP_A = 4
DEEP_B = 5
NA = 20
NB = 32 - NA
BLK = 4
PARAMS = 160
MID = 2 * NA + 120
SCALE = 0.05**0.5
LAG = 4


VMEM = pltpu.VMEM
ANY = pl.ANY
WHOLE = pl.BlockSpec(memory_space=pltpu.VMEM)
SCALAR = pl.BlockSpec(memory_space=pltpu.SMEM)


def split(value):
    high = value.astype(jnp.bfloat16)
    low = (value - high.astype(jnp.float32)).astype(jnp.bfloat16)
    return high, low


def strided_row(ref, base, row, stride):
    parts = [ref[pl.ds(base + start * stride + row, 8, stride=stride), :] for start in STARTS]
    return jnp.concatenate(parts, 0)


def strided_store(ref, row, value):
    for k, start in enumerate(STARTS):
        ref[pl.ds(start * 8 + row, 8, stride=8), :] = value[8 * k : 8 * k + 8]


def first_rows(depth, up_ref, base_up, own_ref, down_ref, base_down):
    def first_row(row):
        if row < depth:
            return strided_row(up_ref, base_up, row, depth)
        if row < depth + 8:
            return strided_row(own_ref, 0, row - depth, 8)
        return strided_row(down_ref, base_down, row - depth - 8, depth)

    return first_row


def emit_pair(member, step, pair, coef, heat, lefts, depth):
    first_row, state, store_last = member
    row = step + 2 * pair
    last = step == STEPS
    shift = DEEP_B - depth

    def load(at):
        if step == 1:
            return first_row(at)
        return state[step % 2][pl.ds(at * 32, 32), :]

    rows = [load(at) for at in range(row - 1, row + 3)]
    smooth = []
    for i in (0, 1):
        here = rows[i + 1]
        at = row + i + shift
        total = (rows[i] + rows[i + 2]) + (pltpu.roll(here, 1, 1) + pltpu.roll(here, 127, 1))
        keep = coef[0, pl.ds(at * 8, 8), :]
        diff = coef[1, pl.ds(at * 8, 8), :]
        smooth.append(jnp.concatenate([keep] * 4, 0) * here + jnp.concatenate([diff] * 4, 0) * total)
    high, low = split(jnp.concatenate(smooth, 1))
    right = jnp.concatenate([high, high, low], 0)
    mixed = jnp.dot(lefts[0 if step == 1 else 2 if last else 1], right, preferred_element_type=jnp.float32)
    for i in (0, 1):
        at = row + i
        part = mixed[:, 128 * i : 128 * (i + 1)]
        warm = heat[1 if last else 0, pl.ds((at + shift) * 32, 32), :]
        if last:
            store_last(at - depth, part * (1.0 - 0.05 * (part * part)) + warm)
        else:
            state[(step + 1) % 2][pl.ds(at * 32, 32), :] = part * (1.0 - part * part) + warm


def run_members(members, coef, heat, lefts, depth):
    count = {step: depth + 4 - step for step in range(1, STEPS + 1)}
    for wave in range(count[1] + LAG * (STEPS - 1) + 1):
        for step in range(1, STEPS + 1):
            pair = wave - LAG * (step - 1)
            if 0 <= pair < count[step]:
                for member in members:
                    emit_pair(member, step, pair, coef, heat, lefts, depth)


def prepare(pup_ref, pdown_ref, hown_ref, diff_ref, mix_ref, coef, heat, lefts):
    for row in range(18):
        if row < 5:
            value = strided_row(pup_ref, 0, row, 5)
            diff = pup_ref[pl.ds(150 + row, 1), :]
        elif row < 13:
            value = strided_row(hown_ref, 0, row - 5, 8)
            diff = diff_ref[pl.ds(row - 5, 1), :]
        else:
            value = strided_row(pdown_ref, 0, row - 13, 5)
            diff = pdown_ref[pl.ds(150 + row - 13, 1), :]
        heat[1, pl.ds(row * 32, 32), :] = value
        heat[0, pl.ds(row * 32, 32), :] = SCALE * value
        diff = jnp.broadcast_to(diff, (8, 128))
        coef[1, pl.ds(row * 8, 8), :] = diff
        coef[0, pl.ds(row * 8, 8), :] = 1.0 - 4.0 * diff
    mix = mix_ref[...]
    for i, factor in enumerate((SCALE, 1.0, 1.0 / SCALE)):
        high, low = split(factor * mix)
        lefts[i] = jnp.concatenate([high, low, high], 1)


def keep_scored(tq_ref, j, out):
    tq_ref[j, 0:8, :] = out[0:8, :]
    tq_ref[j, 8:16, :] = out[8 * LEV : 8 * LEV + 8, :]


def chunk_a_kernel(
    f_ref, up_ref, down_ref, pup_ref, pdown_ref, hown_ref, diff_ref, mix_ref, out_ref, tq_ref, coef, heat, lefts, *states
):
    @pl.when(pl.program_id(0) == 0)
    def _():
        prepare(pup_ref, pdown_ref, hown_ref, diff_ref, mix_ref, coef, heat, lefts)

    def one(p, carry):
        members = []
        for q in range(2):
            j = p * 2 + q
            base = pl.multiple_of(j * 120, 8)
            rows = first_rows(DEEP_A, up_ref, base, f_ref.at[j], down_ref, base)
            members.append((rows, states[2 * q : 2 * q + 2], functools.partial(strided_store, out_ref.at[j])))
        run_members(members, coef, heat, lefts, DEEP_A)
        for q in range(2):
            keep_scored(tq_ref, p * 2 + q, out_ref.at[p * 2 + q])
        return carry

    lax.fori_loop(0, BLK // 2, one, 0)


def chunk_b_kernel(
    killed_ref, f_ref, up_ref, down_ref, dup_ref, ddown_ref, donor_ref, pup_ref, pdown_ref, hown_ref, diff_ref, mix_ref, prev_ref,
    out_ref, tq_ref, edge_ref, coef, heat, lefts, s0, s1, s2, s3, final, donor, sems,
):
    i = pl.program_id(0)
    states = (s0, s1, s2, s3)

    def copy(m, source):
        return pltpu.make_async_copy(source, out_ref.at[m], sems.at[m])

    @pl.when(i == 0)
    def _():
        prepare(pup_ref, pdown_ref, hown_ref, diff_ref, mix_ref, coef, heat, lefts)
        rows = first_rows(DEEP_A, dup_ref, 2 * NA, donor_ref, ddown_ref, 2 * NA)
        run_members([(rows, states[:2], functools.partial(strided_store, donor))], coef, heat, lefts, DEEP_A)
        for m in range(NA):
            @pl.when(killed_ref[m] > 0)
            def _():
                copy(m, donor).start()

    def store_last(j, out, row, value):
        if 0 <= row < 8:
            strided_store(out, row, value)
            return
        slot = 0 if row < 0 else 3
        t, q = value[0:1], value[LEV : LEV + 1]
        edge_ref[j, slot : slot + 1, :] = t
        edge_ref[j, slot + 1 : slot + 2, :] = q
        edge_ref[j, slot + 2 : slot + 3, :] = t

    def one(p, carry):
        members = []
        for q in range(2):
            j = p * 2 + q
            base = j * (30 * DEEP_B)
            out = final.at[i * BLK + j]
            rows = first_rows(DEEP_B, up_ref, base, f_ref.at[j], down_ref, base)
            edge_ref[j] = jnp.zeros((8, 128), jnp.float32)
            members.append((rows, states[2 * q : 2 * q + 2], functools.partial(store_last, j, out)))
        run_members(members, coef, heat, lefts, DEEP_B)
        for q in range(2):
            j = p * 2 + q
            at = i * BLK + j
            m = NA + at
            keep_scored(tq_ref, j, final.at[at])

            @pl.when(killed_ref[m] > 0)
            def _():
                copy(m, donor).start()

            @pl.when(killed_ref[m] <= 0)
            def _():
                copy(m, final.at[at]).start()

        return carry

    lax.fori_loop(0, BLK // 2, one, 0)

    @pl.when(i == pl.num_programs(0) - 1)
    def _():
        for m in range(32):
            if m < NA:
                @pl.when(killed_ref[m] > 0)
                def _():
                    copy(m, donor).wait()
            else:
                copy(m, donor).wait()


def send_rows(x_ref, up_ref, down_ref, base, depth):
    for row in range(depth):
        for start in STARTS:
            to = pl.ds(base + start * depth + row, 8, stride=depth)
            down_ref[to, :] = x_ref[pl.ds(start * 8 + row, 8, stride=8), :]
            up_ref[to, :] = x_ref[pl.ds(start * 8 + 8 - depth + row, 8, stride=8), :]


def send_members(f_ref, first, count, depth, up_ref, down_ref, buf, sems, before):
    fetches = [
        pltpu.make_async_copy(f_ref.at[pl.ds(first + k * BLK, BLK)], buf.at[pl.ds(k * BLK, BLK)], sems.at[k])
        for k in range(count // BLK)
    ]
    for fetch in fetches:
        fetch.start()
    before()

    for k, fetch in enumerate(fetches):
        fetch.wait()

        def one(j, carry):
            m = k * BLK + j
            send_rows(buf.at[m], up_ref, down_ref, m * (30 * depth), depth)
            return carry

        lax.fori_loop(0, BLK, one, 0)


def edges_a_kernel(me_ref, counts_ref, f_ref, heat_ref, diff_ref, land_ref, pieces_ref, up_ref, down_ref, buf, sems, hot_sem):
    me = me_ref[0]
    hot = lax.fori_loop(0, 32, lambda j, at: jnp.where(counts_ref[me * 32 + j] >= 2, j, at), 0)
    fetch = pltpu.make_async_copy(f_ref.at[hot], pieces_ref.at[pl.ds(0, 240)], hot_sem)
    fetch.start()

    def before():
        pieces_ref[240:256, :] = jnp.zeros((16, 128), jnp.float32)
        base = NA * 120
        send_rows(heat_ref, up_ref, down_ref, base, 5)
        diff = diff_ref[...]
        land = land_ref[...].astype(jnp.float32)
        up_ref[base + 150 : base + 155, :] = diff[3:]
        up_ref[base + 155 : base + 160, :] = land[3:]
        down_ref[base + 150 : base + 155, :] = diff[:5]
        down_ref[base + 155 : base + 160, :] = land[:5]

    send_members(f_ref, 0, NA, DEEP_A, up_ref, down_ref, buf, sems, before)
    fetch.wait()


def edges_b_kernel(f_ref, up_ref, down_ref, buf, sems):
    send_members(f_ref, NA, NB, DEEP_B, up_ref, down_ref, buf, sems, lambda: None)


def mid_kernel(donor_ref, tq_ref, up_ref, down_ref):
    for k in range(2 * NA // 8):
        up_ref[pl.ds(8 * k, 8), :] = tq_ref[pl.ds(64 * k + 7, 8, stride=8), :]
        down_ref[pl.ds(8 * k, 8), :] = tq_ref[pl.ds(64 * k, 8, stride=8), :]
    send_rows(donor_ref, up_ref, down_ref, 2 * NA, DEEP_A)


def pick_kernel(index_ref, pieces_ref, out_ref):
    for g in range(16):
        out_ref[g] = pieces_ref[index_ref[g]]


def edge_mask(pup_ref, pdown_ref):
    before, after = pup_ref[159:160, :], pdown_ref[155:156, :]
    one = jnp.ones((1, 128), jnp.float32)
    return jnp.concatenate([before, one, 1.0 - before, after, one, 1.0 - after, one, one], 0)


def score_members(count, tq_ref, edge_ref, land_ref, mask, weight_ref, head_ref, acc, first):
    land = land_ref[...].astype(jnp.float32)
    sea = 1.0 - land
    high, low = split(weight_ref[...])
    left = jnp.concatenate([high, low, high], 1)

    def pair(p, carry):
        cols = []
        for q in range(2):
            m = p * 2 + q
            t = tq_ref[m, 0:8, :]
            edge = edge_ref[pl.ds(pl.multiple_of(m * 8, 8), 8), :]
            value = jnp.concatenate([t * land, tq_ref[m, 8:16, :], t * sea, edge * mask], 0)
            cols.append(jnp.concatenate([pltpu.roll(value, 1, 1), value, pltpu.roll(value, 127, 1)], 0))
        h, l = split(jnp.concatenate(cols, 1))
        right = jnp.concatenate([h, h, l], 0)
        hidden = jnp.maximum(jnp.dot(left, right, preferred_element_type=jnp.float32), 0.0)
        head = head_ref[...]
        for q in range(2):
            part = (hidden[:, 128 * q : 128 * (q + 1)] * head).reshape(32, 8, 128)
            acc[pl.ds(first + p * 2 + q, 1), :] = jnp.sum(jnp.sum(part, 0), 0, keepdims=True)
        return carry

    lax.fori_loop(0, count // 2, pair, 0)


def score_a_kernel(tq_ref, before_ref, after_ref, pup_ref, pdown_ref, land_ref, weight_ref, head_ref, out_ref, edge):
    zero = jnp.zeros((8, 128), jnp.float32)
    for k in range((NA + 7) // 8):
        rows = [ref[pl.ds(16 * k + i, 8, stride=2), :] for ref in (before_ref, after_ref) for i in (0, 1)]
        for slot, value in enumerate((rows[0], rows[1], rows[0], rows[2], rows[3], rows[2], zero, zero)):
            edge[pl.ds(64 * k + slot, 8, stride=8), :] = value
    score_members(NA, tq_ref, edge, land_ref, edge_mask(pup_ref, pdown_ref), weight_ref, head_ref, out_ref, 0)


def score_b_kernel(tq_ref, edge_ref, pup_ref, pdown_ref, land_ref, weight_ref, head_ref, sums_ref, out_ref, acc):
    acc[0:NA, :] = sums_ref[...]
    score_members(NB, tq_ref, edge_ref, land_ref, edge_mask(pup_ref, pdown_ref), weight_ref, head_ref, acc, NA)
    ones = jnp.ones((8, 128), jnp.float32)
    padded = jnp.concatenate([acc[...], jnp.zeros((96, 128), jnp.float32)], 0)
    out_ref[...] = lax.dot_general(
        ones, padded, (((1,), (1,)), ((), ())), precision=lax.Precision.HIGHEST, preferred_element_type=jnp.float32
    )


def weight_kernel(me_ref, parts_ref, counts_ref, source_ref, scores_ref, slot_ref):
    me = me_ref[0]
    scores = jnp.sum(parts_ref[...].reshape(8, 16, 128), 0)[:, :32]
    weights = jnp.exp(scores)
    total = jnp.sum(weights)
    weights = weights / (total / 512.0)
    counts = counts_ref[...].astype(jnp.float32)
    group = lax.broadcasted_iota(jnp.int32, (16, 32), 0)
    member = lax.broadcasted_iota(jnp.int32, (16, 32), 1)
    flat = group * 32 + member
    source = source_ref[...]
    mine = group == me
    killed = jnp.logical_and(mine, source != flat)
    donor = jnp.max(jnp.where(killed, source, -1))
    here = flat == donor
    donor_weight = jnp.sum(jnp.where(here, weights, 0.0))
    donor_count = jnp.sum(jnp.where(here, counts, 0.0))
    top = jnp.where(killed, donor_weight, weights)
    under = jnp.where(killed, donor_count, counts)
    share = jnp.where(mine, top / jnp.where(mine, under, 1.0), 0.0)
    own = jnp.where(mine, scores, 0.0)
    scores_ref[...] = jnp.sum(own, 0, keepdims=True)
    slot_ref[...] = jnp.sum(share, 0, keepdims=True)


def spread_matrix():
    table = np.zeros((27, 8, 96), np.float32)
    for k in range(3):
        for a in (-1, 0, 1):
            for b in (-1, 0, 1):
                tap = 9 * k + 3 * (a + 1) + (b + 1)
                for i in range(8):
                    row = i + a
                    if 0 <= row < 8:
                        slot = 8 * k + row
                    elif row < 0:
                        slot = 24 + k
                    else:
                        slot = 27 + k
                    table[tap, i, (b + 1) * 32 + slot] = 1.0
    return table.reshape(27, 8 * 96)


def call(kernel, outs, **kw):
    return pl.pallas_call(kernel, out_shape=outs, **kw)


def f32(*shape):
    return jax.ShapeDtypeStruct(shape, jnp.float32)


def local(fields, diffusion, mixing, heating, land_mask, conv_weight, head_weight, counts, source):
    size = lax.axis_size("lat")
    up = [(i, i + 1) for i in range(size - 1)]
    down = [(i + 1, i) for i in range(size - 1)]
    me = lax.axis_index("grp").reshape(1).astype(jnp.int32)
    counts2 = counts.reshape(16, 32)
    source2 = source.reshape(16, 32)
    f = fields.reshape(32, 240, 128)
    heat = heating.reshape(240, 128)
    hbm = pl.BlockSpec(memory_space=ANY)

    def edge_scratch(count):
        return [VMEM((count, 240, 128), jnp.float32), pltpu.SemaphoreType.DMA((count // BLK,))]

    rows_a = NA * 120 + PARAMS
    pieces, send_up_a, send_down_a = call(
        edges_a_kernel,
        (f32(256, 128), f32(rows_a, 128), f32(rows_a, 128)),
        in_specs=[SCALAR, SCALAR, hbm, WHOLE, WHOLE, WHOLE],
        out_specs=(WHOLE,) * 3,
        scratch_shapes=edge_scratch(NA) + [pltpu.SemaphoreType.DMA],
        name="edges_a",
    )(me, counts, f, heat, diffusion, land_mask)

    pieces = lax.all_to_all(pieces.reshape(16, 16, 128), "grp", 0, 0, tiled=True)
    up_a = lax.ppermute(send_up_a, "lat", up)
    down_a = lax.ppermute(send_down_a, "lat", down)
    flat = jnp.arange(512, dtype=jnp.int32).reshape(16, 32)
    donor_group = jnp.max(jnp.where(source2 != flat, source2 // 32, 0), 1)
    pieces = call(pick_kernel, f32(16, 16, 128), in_specs=[SCALAR, WHOLE], out_specs=WHOLE, name="pick")(donor_group, pieces)
    donor_state = lax.all_to_all(pieces, "grp", 0, 0, tiled=True).reshape(256, 128)

    send_up_b, send_down_b = call(
        edges_b_kernel,
        (f32(NB * 150, 128), f32(NB * 150, 128)),
        in_specs=[hbm],
        out_specs=(WHOLE, WHOLE),
        scratch_shapes=edge_scratch(NB),
        name="edges_b",
    )(f)
    up_b = lax.ppermute(send_up_b, "lat", up)
    down_b = lax.ppermute(send_down_b, "lat", down)

    mix = jnp.concatenate([mixing[:24], mixing[22:]], 0)
    mix = jnp.concatenate([mix[:, :24], jnp.zeros((32, 2), jnp.float32), mix[:, 24:]], 1)
    taps = jnp.dot(conv_weight, jnp.asarray(spread_matrix()), precision=lax.Precision.HIGHEST).reshape(256, 96)
    head = head_weight.reshape(256, 128)
    killed = (lax.dynamic_index_in_dim(counts2, me[0], 0, keepdims=False) == 0).astype(jnp.int32)

    def whole(shape, at=0):
        return pl.BlockSpec(shape, lambda *i: (at,) + (0,) * (len(shape) - 1))

    params = whole((PARAMS, 128), NA * 120 // PARAMS)
    block = pl.BlockSpec((BLK, 240, 128), lambda i: (i, 0, 0))
    tq_block = pl.BlockSpec((BLK, 16, 128), lambda i: (i, 0, 0))
    step_scratch = [
        VMEM((2, 18 * 8, 128), jnp.float32),
        VMEM((2, 18 * 32, 128), jnp.float32),
        VMEM((3, 32, 96), jnp.bfloat16),
    ] + [VMEM((18 * 32, 128), jnp.float32)] * 4
    shared = [params, params, WHOLE, WHOLE, WHOLE]
    halo_a = pl.BlockSpec((BLK * 30 * DEEP_A, 128), lambda i: (i, 0))
    state_a, tq_a = call(
        chunk_a_kernel,
        (f32(32, 240, 128), f32(NA, 16, 128)),
        grid=(NA // BLK,),
        in_specs=[block, halo_a, halo_a] + shared,
        out_specs=(block, tq_block),
        scratch_shapes=step_scratch,
        name="chunk_a",
    )(f, up_a, down_a, up_a, down_a, heat, diffusion, mix)

    send_up, send_down = call(
        mid_kernel, (f32(MID, 128), f32(MID, 128)), in_specs=[WHOLE, WHOLE], out_specs=(WHOLE, WHOLE), name="mid"
    )(donor_state, tq_a.reshape(NA * 16, 128))
    before = lax.ppermute(send_up, "lat", up)
    after = lax.ppermute(send_down, "lat", down)

    sums_a = call(
        score_a_kernel,
        f32(NA, 128),
        grid=(1,),
        in_specs=[WHOLE] * 3 + [params] * 2 + [WHOLE] * 3,
        out_specs=WHOLE,
        scratch_shapes=[VMEM(((NA + 7) // 8 * 64, 128), jnp.float32)],
        name="score_a",
    )(tq_a, before, after, up_a, down_a, land_mask, taps, head)

    halo_b = pl.BlockSpec((BLK * 30 * DEEP_B, 128), lambda i: (i, 0))
    new_fields, tq_b, edge_b = call(
        chunk_b_kernel,
        (f32(32, 240, 128), f32(NB, 16, 128), f32(NB, 8, 128)),
        grid=(NB // BLK,),
        in_specs=[SCALAR, pl.BlockSpec((BLK, 240, 128), lambda i: (i + NA // BLK, 0, 0)), halo_b, halo_b]
        + [WHOLE] * 3
        + shared
        + [hbm],
        out_specs=(hbm, tq_block, pl.BlockSpec((BLK, 8, 128), lambda i: (i, 0, 0))),
        scratch_shapes=step_scratch
        + [VMEM((NB, 240, 128), jnp.float32), VMEM((240, 128), jnp.float32), pltpu.SemaphoreType.DMA((32,))],
        input_output_aliases={12: 0},
        name="chunk_b",
    )(killed, f, up_b, down_b, before, after, donor_state, up_a, down_a, heat, diffusion, mix, state_a)

    partial = call(
        score_b_kernel,
        f32(8, 128),
        grid=(1,),
        in_specs=[WHOLE] * 2 + [params] * 2 + [WHOLE] * 4,
        out_specs=WHOLE,
        scratch_shapes=[VMEM((32, 128), jnp.float32)],
        name="score_b",
    )(tq_b, edge_b.reshape(NB * 8, 128), up_a, down_a, land_mask, taps, head, sums_a)

    parts = lax.all_to_all(jnp.broadcast_to(partial[:1].reshape(1, 1, 128), (128, 1, 128)), ("lat", "grp"), 0, 0, tiled=True)
    scores, slot = call(
        weight_kernel, (f32(1, 32), f32(1, 32)), in_specs=[SCALAR] + [WHOLE] * 3, out_specs=(WHOLE, WHOLE), name="weights"
    )(me, parts.reshape(128, 128), counts2, source2)
    return new_fields.reshape(32, 30, 8, 128), scores.reshape(32), slot.reshape(32)


def solution(mesh):
    return jax.shard_map(
        local,
        mesh=mesh,
        in_specs=(
            P("grp", None, "lat", None),
            P("lat", None),
            P(),
            P(None, "lat", None),
            P("lat", None),
            P(),
            P(None, "lat", None),
            P(),
            P(),
        ),
        out_specs=(P("grp", None, "lat", None), P("grp"), P("grp")),
        check_vma=False,
    )
```

profile of v0, /device:TPU:1, one launch (start us, length us, event | category | flops | bytes accessed | tf_op | source)
XLA Modules:
  0.0 153.8 jit_solution(10905487892908537687)
XLA Ops:
  0.6 0.0 copy-start
  0.6 4.6 %edges_a.1 = (f32[256,128]{1,0:T(8,128)}, f32[2560,128]{1,0:T(8,128)}, f32[2560,128]{1,0:T(8,128)}) custom-call(s32[1]{0:T(128)} %bitcast.2.me_ref, s32[512]{0:T(512)} %counts_ref.1, f32[32,240,128]{2,1,0:T(8,128)} %bitcast.20, f32[240,128]{1,0:T(8,128)} %bitcast.27, f32[8,128]{1,0:T(8,128)} %diff_ref.5, s32[8,128]{1,0:T(8,128)} %land_ref.5), custom_call_target="tpu_custom_call" | custom-call | tf_op jit(solution)/shard_map/edges_a/pallas_call | solution.py:402
  5.3 4.1 %collective-permute-start.2 = (f32[2560,128]{1,0:T(8,128)}, f32[2560,128]{1,0:T(8,128)S(1)}, u32[]{:S(2)}, u32[]{:S(2)}) collective-permute-start(f32[2560,128]{1,0:T(8,128)} %get-tuple-element.20), channel_id=1, source_target_pairs={{0,16},{16,32},{32,48},{48,64},{64,80},{80,96},{96,112},{1,17},{17... | collective-permute-start | bytes 3932168 | tf_op jit(solution)/shard_map/ppermute | solution.py:412
  9.4 0.0 copy-start.10
  9.4 0.0 copy-start.7
  9.4 0.0 copy-start.11
  9.4 0.0 copy-start.12
  9.5 1.4 collective-permute-start.3
  10.9 2.8 %edges_b.1 = (f32[1800,128]{1,0:T(8,128)}, f32[1800,128]{1,0:T(8,128)}) custom-call(f32[32,240,128]{2,1,0:T(8,128)} %bitcast.21), custom_call_target="tpu_custom_call" | custom-call | tf_op jit(solution)/shard_map/edges_b/pallas_call | solution.py:419
  13.7 4.9 %collective-permute-start = (f32[1800,128]{1,0:T(8,128)}, f32[1800,128]{1,0:T(8,128)}, u32[]{:S(2)}, u32[]{:S(2)}) collective-permute-start(f32[1800,128]{1,0:T(8,128)} %get-tuple-element.17), channel_id=1, source_target_pairs={{0,16},{16,32},{32,48},{48,64},{64,80},{80,96},{96,112},{1,17},{17... | collective-permute-start | bytes 2764808 | tf_op jit(solution)/shard_map/ppermute | solution.py:427
  18.6 1.3 collective-permute-start.1
  19.9 7.8 %all-to-all-start = ((f32[16,16,128]{2,1,0:T(8,128)}), f32[16,16,128]{2,1,0:T(8,128)S(1)}, u32[]{:S(2)}, u32[]{:S(2)}) async-start(f32[16,16,128]{2,1,0:T(8,128)} %bitcast.4), calls=%async_computation | async-start | bytes 262144 | tf_op jit(solution)/shard_map/all_to_all | solution.py:411
  27.6 0.0 copy-done.10
  27.7 0.0 copy-done
  27.7 0.0 copy-done.7
  27.7 0.2 convolution_bitcast_fusion
  27.9 0.0 copy-done.11
  28.0 0.1 reshape.66.counts_ref
  28.0 0.0 copy-done.12
  28.0 0.0 copy-start.9
  28.0 0.1 reshape.68.source_ref
  28.1 0.0 copy-start.8
  28.1 0.8 reshape.79.weight_ref
  28.9 0.1 pad.1.clone
  29.0 0.6 fusion.3.index_ref
  29.6 4.2 %all-to-all-done.pieces_ref = f32[16,16,128]{2,1,0:T(8,128)S(1)} async-done(((f32[16,16,128]{2,1,0:T(8,128)}), f32[16,16,128]{2,1,0:T(8,128)S(1)}, u32[]{:S(2)}, u32[]{:S(2)}) %all-to-all-start) | async-done | bytes 131104 | tf_op jit(solution)/shard_map/all_to_all | solution.py:411
  33.8 0.0 copy-start.4
  33.8 0.7 copy-done.4
  34.4 1.6 %pick.1 = f32[16,16,128]{2,1,0:T(8,128)} custom-call(s32[16]{0:T(128)} %fusion.3.index_ref, f32[16,16,128]{2,1,0:T(8,128)} %copy-done.4), custom_call_target="tpu_custom_call" | custom-call | tf_op jit(solution)/shard_map/pick/pallas_call | solution.py:416
  36.0 4.0 %all-to-all-start.1 = ((f32[16,16,128]{2,1,0:T(8,128)}), f32[16,16,128]{2,1,0:T(8,128)S(1)}, u32[]{:S(2)}, u32[]{:S(2)}) async-start(f32[16,16,128]{2,1,0:T(8,128)} %pick.1), calls=%async_computation.1 | async-start | bytes 262144 | tf_op jit(solution)/shard_map/all_to_all | solution.py:417
  40.0 0.7 fusion.mix_ref
  40.6 0.0 collective-permute-done.2.up_ref.pup_ref
  40.6 0.0 copy-start.1
  40.6 0.4 collective-permute-done.3.down_ref.pdown_ref
  41.1 0.6 copy-done.1
  41.7 0.0 copy-start.2
  41.7 1.0 copy-done.2
  42.8 16.0 %chunk_a.1 = (f32[32,240,128]{2,1,0:T(8,128)}, f32[20,16,128]{2,1,0:T(8,128)}) custom-call(f32[32,240,128]{2,1,0:T(8,128)} %bitcast.22, f32[2560,128]{1,0:T(8,128)} %copy-done.1, f32[2560,128]{1,0:T(8,128)} %copy-done.2, f32[2560,128]{1,0:T(8,128)} %copy-done.1, f32[2560,128]{1,0:T(8,128)} %copy-done.2, f32[240,128]{1,0:T(8,128)} %bitcast.28, ...), custom_call_target="tpu_custom_call" | custom-call | tf_op jit(solution)/shard_map/chunk_a/pallas_call | solution.py:449
  58.7 0.0 copy-done.8
  58.7 0.0 all-to-all-done.1
  58.8 0.0 copy-start.3
  58.8 0.6 copy-done.3
  59.4 1.7 %mid.1 = (f32[160,128]{1,0:T(8,128)}, f32[160,128]{1,0:T(8,128)}) custom-call(f32[256,128]{1,0:T(8,128)} %bitcast.25, f32[320,128]{1,0:T(8,128)} %bitcast.30), custom_call_target="tpu_custom_call" | custom-call | tf_op jit(solution)/shard_map/mid/pallas_call | solution.py:459
  61.1 4.3 %collective-permute-start.4 = (f32[160,128]{1,0:T(8,128)}, f32[160,128]{1,0:T(8,128)S(1)}, u32[]{:S(2)}, u32[]{:S(2)}) collective-permute-start(f32[160,128]{1,0:T(8,128)} %get-tuple-element.23), channel_id=1, source_target_pairs={{0,16},{16,32},{32,48},{48,64},{64,80},{80,96},{96,112},{1,17},{17... | collective-permute-start | bytes 245768 | tf_op jit(solution)/shard_map/ppermute | solution.py:462
  65.4 1.3 collective-permute-start.5
  66.7 0.0 copy-done.9
  66.7 0.5 fusion.5.killed_ref
  67.2 0.0 collective-permute-done.4.dup_ref.before_ref
  67.2 0.0 copy-start.5
  67.2 3.6 %collective-permute-done.5.ddown_ref.after_ref = f32[160,128]{1,0:T(8,128)S(1)} collective-permute-done((f32[160,128]{1,0:T(8,128)}, f32[160,128]{1,0:T(8,128)S(1)}, u32[]{:S(2)}, u32[]{:S(2)}) %collective-permute-start.5) | collective-permute-done | bytes 81952 | tf_op jit(solution)/shard_map/ppermute | solution.py:463
  70.8 0.0 copy-start.6
  70.8 0.0 copy-done.5
  70.8 0.6 copy-done.6
  71.4 5.0 %score_a.1.sums_ref = f32[20,128]{1,0:T(8,128)} custom-call(f32[20,16,128]{2,1,0:T(8,128)} %get-tuple-element.22.tq_ref, f32[160,128]{1,0:T(8,128)} %copy-done.5, f32[160,128]{1,0:T(8,128)} %copy-done.6, f32[2560,128]{1,0:T(8,128)} %copy-done.1, f32[2560,128]{1,0:T(8,128)} %copy-done.2, s32[8,128]{1,0:T(8,128)} %land_ref.5, f32[256,96]{1,0:T(8,128)} %reshape.79.weight_ref, ...), custom_call_target="tpu_custom_call" | custom-call | tf_op jit(solution)/shard_map/score_a/pallas_call | solution.py:465
  76.4 0.0 collective-permute-done.up_ref
  76.4 0.0 collective-permute-done.1.down_ref
  76.4 12.8 %chunk_b.1 = (f32[32,240,128]{2,1,0:T(8,128)}, f32[12,16,128]{2,1,0:T(8,128)}, f32[12,8,128]{2,1,0:T(8,128)}) custom-call(s32[32]{0:T(128)} %fusion.5.killed_ref, f32[32,240,128]{2,1,0:T(8,128)} %bitcast.23, f32[1800,128]{1,0:T(8,128)} %collective-permute-done.up_ref, f32[1800,128]{1,0:T(8,128)} %collective-permute-done.1.down_ref, ...), custom_call_target="tpu_custom_call", output_to_operand_aliasing={{0}: (12, {})} | custom-call | tf_op jit(solution)/shard_map/chunk_b/pallas_call | solution.py:476
  89.2 3.8 %score_b.1 = f32[8,128]{1,0:T(8,128)} custom-call(f32[12,16,128]{2,1,0:T(8,128)} %get-tuple-element.27.tq_ref, f32[96,128]{1,0:T(8,128)} %bitcast.34, f32[2560,128]{1,0:T(8,128)} %copy-done.1, f32[2560,128]{1,0:T(8,128)} %copy-done.2, s32[8,128]{1,0:T(8,128)} %land_ref.5, f32[256,96]{1,0:T(8,128)} %reshape.79.weight_ref, f32[256,128]{1,0:T(8,128)} %bitcast.32, ...), custom_call_target="tpu_custom_call" | custom-call | tf_op jit(solution)/shard_map/score_b/pallas_call | solution.py:491
  93.0 0.7 slice_bitcast_fusion
  93.7 58.3 %all_to_all.15 = f32[128,1,128]{2,1,0:T(1,128)} all-to-all(f32[128,1,128]{2,1,0:T(1,128)S(1)} %broadcast_in_dim.14), channel_id=1, replica_groups=mesh['lat'=8,'grp'=16] {'lat','grp'}, dimensions={0} | all-to-all | bytes 131072 | tf_op jit(solution)/shard_map/all_to_all | solution.py:501
  152.0 1.7 %weights.1 = (f32[1,32]{1,0:T(1,128)}, f32[1,32]{1,0:T(1,128)}) custom-call(s32[1]{0:T(128)} %bitcast.2.me_ref, f32[128,128]{1,0:T(8,128)} %bitcast.33, s32[16,32]{1,0:T(8,128)} %copy-done.9, s32[16,32]{1,0:T(8,128)} %copy-done.8), custom_call_target="tpu_custom_call" | custom-call | tf_op jit(solution)/shard_map/weights/pallas_call | solution.py:502
  (5 shorter events, 0.1 us)
Async XLA Ops:
  0.6 27.0 %copy-start = (f32[32,27]{1,0:T(8,128)S(1)}, f32[32,27]{1,0:T(8,128)}, u32[]{:S(2)}) copy-start(f32[32,27]{1,0:T(8,128)} %param.15) | copy-start | bytes 10372
  5.3 35.3 %collective-permute-start.2 = (f32[2560,128]{1,0:T(8,128)}, f32[2560,128]{1,0:T(8,128)S(1)}, u32[]{:S(2)}, u32[]{:S(2)}) collective-permute-start(f32[2560,128]{1,0:T(8,128)} %get-tuple-element.20), channel_id=1, source_target_pairs={{0,16},{16,32},{32,48},{48,64},{64,80},{80,96},{96,112},{1,17},{17... | collective-permute-start | bytes 3932168 | tf_op jit(solution)/shard_map/ppermute | solution.py:412
  9.4 18.2 %copy-start.10 = (f32[30,30]{1,0:T(8,128)S(1)}, f32[30,30]{1,0:T(8,128)}, u32[]{:S(2)}) copy-start(f32[30,30]{1,0:T(8,128)} %param.12) | copy-start | bytes 10804
  9.4 18.3 %copy-start.7 = (f32[27,768]{1,0:T(8,128)S(1)}, f32[27,768]{1,0:T(8,128)}, u32[]{:S(2)}) copy-start(f32[27,768]{1,0:T(8,128)} %constant.35.clone) | copy-start | bytes 248836
  9.4 18.5 %copy-start.11 = (s32[512]{0:T(512)S(1)}, s32[512]{0:T(512)}, u32[]{:S(2)}) copy-start(s32[512]{0:T(512)} %counts_ref.1) | copy-start | bytes 6148
  9.4 18.6 %copy-start.12 = (s32[512]{0:T(512)S(1)}, s32[512]{0:T(512)}, u32[]{:S(2)}) copy-start(s32[512]{0:T(512)} %param.18) | copy-start | bytes 6148
  9.5 31.6 %collective-permute-start.3 = (f32[2560,128]{1,0:T(8,128)}, f32[2560,128]{1,0:T(8,128)S(1)}, u32[]{:S(2)}, u32[]{:S(2)}) collective-permute-start(f32[2560,128]{1,0:T(8,128)} %get-tuple-element.21), channel_id=1, source_target_pairs={{16,0},{32,16},{48,32},{64,48},{80,64},{96,80},{112,96},{17,1},{33... | collective-permute-start | bytes 3932168 | tf_op jit(solution)/shard_map/ppermute | solution.py:413
  13.7 62.7 %collective-permute-start = (f32[1800,128]{1,0:T(8,128)}, f32[1800,128]{1,0:T(8,128)}, u32[]{:S(2)}, u32[]{:S(2)}) collective-permute-start(f32[1800,128]{1,0:T(8,128)} %get-tuple-element.17), channel_id=1, source_target_pairs={{0,16},{16,32},{32,48},{48,64},{64,80},{80,96},{96,112},{1,17},{17... | collective-permute-start | bytes 2764808 | tf_op jit(solution)/shard_map/ppermute | solution.py:427
  18.6 57.8 %collective-permute-start.1 = (f32[1800,128]{1,0:T(8,128)}, f32[1800,128]{1,0:T(8,128)}, u32[]{:S(2)}, u32[]{:S(2)}) collective-permute-start(f32[1800,128]{1,0:T(8,128)} %get-tuple-element.18), channel_id=1, source_target_pairs={{16,0},{32,16},{48,32},{64,48},{80,64},{96,80},{112,96},{17,1},{33... | collective-permute-start | bytes 2764808 | tf_op jit(solution)/shard_map/ppermute | solution.py:428
  19.9 13.9 %all-to-all-start = ((f32[16,16,128]{2,1,0:T(8,128)}), f32[16,16,128]{2,1,0:T(8,128)S(1)}, u32[]{:S(2)}, u32[]{:S(2)}) async-start(f32[16,16,128]{2,1,0:T(8,128)} %bitcast.4), calls=%async_computation | async-start | bytes 262144 | tf_op jit(solution)/shard_map/all_to_all | solution.py:411
  28.0 38.6 %copy-start.9 = (s32[16,32]{1,0:T(8,128)}, s32[16,32]{1,0:T(8,128)S(1)}, u32[]{:S(2)}) copy-start(s32[16,32]{1,0:T(8,128)S(1)} %reshape.66.counts_ref) | copy-start | bytes 6148
  28.1 30.6 %copy-start.8 = (s32[16,32]{1,0:T(8,128)}, s32[16,32]{1,0:T(8,128)S(1)}, u32[]{:S(2)}) copy-start(s32[16,32]{1,0:T(8,128)S(1)} %reshape.68.source_ref) | copy-start | bytes 6148
  33.8 0.7 copy-start.4
  36.0 22.7 %all-to-all-start.1 = ((f32[16,16,128]{2,1,0:T(8,128)}), f32[16,16,128]{2,1,0:T(8,128)S(1)}, u32[]{:S(2)}, u32[]{:S(2)}) async-start(f32[16,16,128]{2,1,0:T(8,128)} %pick.1), calls=%async_computation.1 | async-start | bytes 262144 | tf_op jit(solution)/shard_map/all_to_all | solution.py:417
  40.6 1.1 copy-start.1
  41.7 1.1 copy-start.2
  58.8 0.7 copy-start.3
  61.1 6.1 %collective-permute-start.4 = (f32[160,128]{1,0:T(8,128)}, f32[160,128]{1,0:T(8,128)S(1)}, u32[]{:S(2)}, u32[]{:S(2)}) collective-permute-start(f32[160,128]{1,0:T(8,128)} %get-tuple-element.23), channel_id=1, source_target_pairs={{0,16},{16,32},{32,48},{48,64},{64,80},{80,96},{96,112},{1,17},{17... | collective-permute-start | bytes 245768 | tf_op jit(solution)/shard_map/ppermute | solution.py:462
  65.4 5.4 %collective-permute-start.5 = (f32[160,128]{1,0:T(8,128)}, f32[160,128]{1,0:T(8,128)S(1)}, u32[]{:S(2)}, u32[]{:S(2)}) collective-permute-start(f32[160,128]{1,0:T(8,128)} %get-tuple-element.24), channel_id=1, source_target_pairs={{16,0},{32,16},{48,32},{64,48},{80,64},{96,80},{112,96},{17,1},{33... | collective-permute-start | bytes 245768 | tf_op jit(solution)/shard_map/ppermute | solution.py:463
  67.2 3.6 %copy-start.5 = (f32[160,128]{1,0:T(8,128)}, f32[160,128]{1,0:T(8,128)S(1)}, u32[]{:S(2)}) copy-start(f32[160,128]{1,0:T(8,128)S(1)} %collective-permute-done.4.dup_ref.before_ref) | copy-start | bytes 245764
  70.8 0.6 copy-start.6
where the time goes:
time: 154 us
  blocking collectives  58.3 us (38%)
  Pallas kernels  49.9 us (32%)
  starting transfers between devices  29 us (19%)
  waiting for transfers between devices  8.18 us (5%)
  local copies, waits for them, and re-layouts  5.38 us (3%)
  other arithmetic  1.84 us (1%)
    all_to_all x1, blocking collectives, local(): lax.all_to_all(jnp.broadcast_to(partial[:1].reshape(1, 1, 128), (128, 1,...  58.3 us
    pallas_call x1, Pallas kernels, local(): call(chunk_a_kernel, (f32(32, 240, 128), f32(NA, 16, 128)), grid=(NA // B...  16 us
    pallas_call x1, Pallas kernels, local(): call(chunk_b_kernel, (f32(32, 240, 128), f32(NB, 16, 128), f32(NB, 8, 128...  12.8 us
    all_to_all x1, starting transfers between devices, local(): lax.all_to_all(pieces.reshape(16, 16, 128), 'grp', 0, 0, tiled=True)  7.78 us
    pallas_call x1, Pallas kernels, local(): call(score_a_kernel, f32(NA, 128), grid=(1,), in_specs=[WHOLE] * 3 + [par...  4.97 us
    ppermute x1, starting transfers between devices, local(): up_b = lax.ppermute(send_up_b, 'lat', up)  4.92 us
    pallas_call x1, Pallas kernels, local(): call(edges_a_kernel, (f32(256, 128), f32(rows_a, 128), f32(rows_a, 128)),...  4.64 us
    ppermute x1, starting transfers between devices, local(): before = lax.ppermute(send_up, 'lat', up)  4.26 us
  transfers between devices with their start and end apart: 8, of which 3 were waited for; matrix products, arithmetic and copies ran while one was open for 2% of the time, Pallas kernels for 18%

commit v1 on v0

--- a/solution.py
+++ b/solution.py
@@ -149,28 +149,16 @@
 
 
 def chunk_b_kernel(
-    killed_ref, f_ref, up_ref, down_ref, dup_ref, ddown_ref, donor_ref, pup_ref, pdown_ref, hown_ref, diff_ref, mix_ref, prev_ref,
-    out_ref, tq_ref, edge_ref, coef, heat, lefts, s0, s1, s2, s3, final, donor, sems,
+    f_ref, up_ref, down_ref, pup_ref, pdown_ref, hown_ref, diff_ref, mix_ref, prev_ref, out_ref, tq_ref, edge_ref, coef, heat, lefts,
+    *states,
 ):
-    i = pl.program_id(0)
-    states = (s0, s1, s2, s3)
-
-    def copy(m, source):
-        return pltpu.make_async_copy(source, out_ref.at[m], sems.at[m])
-
-    @pl.when(i == 0)
+    @pl.when(pl.program_id(0) == 0)
     def _():
         prepare(pup_ref, pdown_ref, hown_ref, diff_ref, mix_ref, coef, heat, lefts)
-        rows = first_rows(DEEP_A, dup_ref, 2 * NA, donor_ref, ddown_ref, 2 * NA)
-        run_members([(rows, states[:2], functools.partial(strided_store, donor))], coef, heat, lefts, DEEP_A)
-        for m in range(NA):
-            @pl.when(killed_ref[m] > 0)
-            def _():
-                copy(m, donor).start()
-
-    def store_last(j, out, row, value):
+
+    def store_last(j, row, value):
         if 0 <= row < 8:
-            strided_store(out, row, value)
+            strided_store(out_ref.at[j], row, value)
             return
         slot = 0 if row < 0 else 3
         t, q = value[0:1], value[LEV : LEV + 1]
@@ -183,38 +171,15 @@
         for q in range(2):
             j = p * 2 + q
             base = j * (30 * DEEP_B)
-            out = final.at[i * BLK + j]
             rows = first_rows(DEEP_B, up_ref, base, f_ref.at[j], down_ref, base)
             edge_ref[j] = jnp.zeros((8, 128), jnp.float32)
-            members.append((rows, states[2 * q : 2 * q + 2], functools.partial(store_last, j, out)))
+            members.append((rows, states[2 * q : 2 * q + 2], functools.partial(store_last, j)))
         run_members(members, coef, heat, lefts, DEEP_B)
         for q in range(2):
-            j = p * 2 + q
-            at = i * BLK + j
-            m = NA + at
-            keep_scored(tq_ref, j, final.at[at])
-
-            @pl.when(killed_ref[m] > 0)
-            def _():
-                copy(m, donor).start()
-
-            @pl.when(killed_ref[m] <= 0)
-            def _():
-                copy(m, final.at[at]).start()
-
+            keep_scored(tq_ref, p * 2 + q, out_ref.at[p * 2 + q])
         return carry
 
     lax.fori_loop(0, BLK // 2, one, 0)
-
-    @pl.when(i == pl.num_programs(0) - 1)
-    def _():
-        for m in range(32):
-            if m < NA:
-                @pl.when(killed_ref[m] > 0)
-                def _():
-                    copy(m, donor).wait()
-            else:
-                copy(m, donor).wait()
 
 
 def send_rows(x_ref, up_ref, down_ref, base, depth):
@@ -225,27 +190,42 @@
             up_ref[to, :] = x_ref[pl.ds(start * 8 + 8 - depth + row, 8, stride=8), :]
 
 
-def send_members(f_ref, first, count, depth, up_ref, down_ref, buf, sems, before):
+def send_members(f_ref, first, count, depth, up_ref, down_ref, buf, up_buf, down_buf, sems, before):
+    rows = BLK * 30 * depth
+    blocks = count // BLK
     fetches = [
-        pltpu.make_async_copy(f_ref.at[pl.ds(first + k * BLK, BLK)], buf.at[pl.ds(k * BLK, BLK)], sems.at[k])
-        for k in range(count // BLK)
+        pltpu.make_async_copy(f_ref.at[pl.ds(first + k * BLK, BLK)], buf.at[pl.ds(k * BLK, BLK)], sems.at[k]) for k in range(blocks)
     ]
     for fetch in fetches:
         fetch.start()
-    before()
-
+    copies = []
+
+    def put(start, size, k):
+        for i, (source, target) in enumerate(((up_buf, up_ref), (down_buf, down_ref))):
+            where = pl.ds(start, size)
+            copies.append(pltpu.make_async_copy(source.at[where], target.at[where], sems.at[blocks + 2 * k + i]))
+            copies[-1].start()
+
+    extra = before()
+    if extra:
+        put(count * 30 * depth, extra, blocks)
     for k, fetch in enumerate(fetches):
         fetch.wait()
 
         def one(j, carry):
             m = k * BLK + j
-            send_rows(buf.at[m], up_ref, down_ref, m * (30 * depth), depth)
+            send_rows(buf.at[m], up_buf, down_buf, m * (30 * depth), depth)
             return carry
 
         lax.fori_loop(0, BLK, one, 0)
-
-
-def edges_a_kernel(me_ref, counts_ref, f_ref, heat_ref, diff_ref, land_ref, pieces_ref, up_ref, down_ref, buf, sems, hot_sem):
+        put(k * rows, rows, k)
+    for copy in copies:
+        copy.wait()
+
+
+def edges_a_kernel(
+    me_ref, counts_ref, f_ref, heat_ref, diff_ref, land_ref, pieces_ref, up_ref, down_ref, buf, up_buf, down_buf, sems, hot_sem
+):
     me = me_ref[0]
     hot = lax.fori_loop(0, 32, lambda j, at: jnp.where(counts_ref[me * 32 + j] >= 2, j, at), 0)
     fetch = pltpu.make_async_copy(f_ref.at[hot], pieces_ref.at[pl.ds(0, 240)], hot_sem)
@@ -254,20 +234,21 @@
     def before():
         pieces_ref[240:256, :] = jnp.zeros((16, 128), jnp.float32)
         base = NA * 120
-        send_rows(heat_ref, up_ref, down_ref, base, 5)
+        send_rows(heat_ref, up_buf, down_buf, base, 5)
         diff = diff_ref[...]
         land = land_ref[...].astype(jnp.float32)
-        up_ref[base + 150 : base + 155, :] = diff[3:]
-        up_ref[base + 155 : base + 160, :] = land[3:]
-        down_ref[base + 150 : base + 155, :] = diff[:5]
-        down_ref[base + 155 : base + 160, :] = land[:5]
-
-    send_members(f_ref, 0, NA, DEEP_A, up_ref, down_ref, buf, sems, before)
+        up_buf[base + 150 : base + 155, :] = diff[3:]
+        up_buf[base + 155 : base + 160, :] = land[3:]
+        down_buf[base + 150 : base + 155, :] = diff[:5]
+        down_buf[base + 155 : base + 160, :] = land[:5]
+        return PARAMS
+
+    send_members(f_ref, 0, NA, DEEP_A, up_ref, down_ref, buf, up_buf, down_buf, sems, before)
     fetch.wait()
 
 
-def edges_b_kernel(f_ref, up_ref, down_ref, buf, sems):
-    send_members(f_ref, NA, NB, DEEP_B, up_ref, down_ref, buf, sems, lambda: None)
+def edges_b_kernel(f_ref, up_ref, down_ref, buf, up_buf, down_buf, sems):
+    send_members(f_ref, NA, NB, DEEP_B, up_ref, down_ref, buf, up_buf, down_buf, sems, lambda: 0)
 
 
 def mid_kernel(donor_ref, tq_ref, up_ref, down_ref):
@@ -288,49 +269,76 @@
     return jnp.concatenate([before, one, 1.0 - before, after, one, 1.0 - after, one, one], 0)
 
 
-def score_members(count, tq_ref, edge_ref, land_ref, mask, weight_ref, head_ref, acc, first):
-    land = land_ref[...].astype(jnp.float32)
+def score_members(count, tq_ref, edge_ref, land, mask, left, head_ref, acc, first):
     sea = 1.0 - land
-    high, low = split(weight_ref[...])
-    left = jnp.concatenate([high, low, high], 1)
-
-    def pair(p, carry):
-        cols = []
-        for q in range(2):
-            m = p * 2 + q
-            t = tq_ref[m, 0:8, :]
-            edge = edge_ref[pl.ds(pl.multiple_of(m * 8, 8), 8), :]
-            value = jnp.concatenate([t * land, tq_ref[m, 8:16, :], t * sea, edge * mask], 0)
-            cols.append(jnp.concatenate([pltpu.roll(value, 1, 1), value, pltpu.roll(value, 127, 1)], 0))
-        h, l = split(jnp.concatenate(cols, 1))
-        right = jnp.concatenate([h, h, l], 0)
-        hidden = jnp.maximum(jnp.dot(left, right, preferred_element_type=jnp.float32), 0.0)
-        head = head_ref[...]
-        for q in range(2):
-            part = (hidden[:, 128 * q : 128 * (q + 1)] * head).reshape(32, 8, 128)
-            acc[pl.ds(first + p * 2 + q, 1), :] = jnp.sum(jnp.sum(part, 0), 0, keepdims=True)
+
+    def four(p, carry):
+        rights = []
+        for pair in range(2):
+            cols = []
+            for q in range(2):
+                m = p * 4 + pair * 2 + q
+                t = tq_ref[m, 0:8, :]
+                edge = edge_ref[pl.ds(pl.multiple_of(m * 8, 8), 8), :]
+                value = jnp.concatenate([t * land, tq_ref[m, 8:16, :], t * sea, edge * mask], 0)
+                cols.append(jnp.concatenate([pltpu.roll(value, 1, 1), value, pltpu.roll(value, 127, 1)], 0))
+            h, l = split(jnp.concatenate(cols, 1))
+            rights.append(jnp.concatenate([h, h, l], 0))
+        for pair in range(2):
+            total = [jnp.zeros((8, 128), jnp.float32)] * 2
+            for block in range(4):
+                rows = slice(64 * block, 64 * block + 64)
+                hidden = jnp.maximum(jnp.dot(left[rows, :], rights[pair], preferred_element_type=jnp.float32), 0.0)
+                head = head_ref[rows, :]
+                for q in range(2):
+                    part = (hidden[:, 128 * q : 128 * (q + 1)] * head).reshape(8, 8, 128)
+                    total[q] = total[q] + jnp.sum(part, 0)
+            for q in range(2):
+                acc[pl.ds(first + p * 4 + pair * 2 + q, 1), :] = jnp.sum(total[q], 0, keepdims=True)
         return carry
 
-    lax.fori_loop(0, count // 2, pair, 0)
-
-
-def score_a_kernel(tq_ref, before_ref, after_ref, pup_ref, pdown_ref, land_ref, weight_ref, head_ref, out_ref, edge):
+    lax.fori_loop(0, count // 4, four, 0)
+
+
+def finish_kernel(
+    killed_ref, tqa_ref, before_ref, after_ref, tqb_ref, edgeb_ref, land_ref, weight_ref, head_ref, donor_ref,
+    pup_ref, pdown_ref, hown_ref, diff_ref, mix_ref, prev_ref,
+    out_ref, sums_ref, coef, heat, lefts, s0, s1, donor, edge, left, acc, sems,
+):
+    prepare(pup_ref, pdown_ref, hown_ref, diff_ref, mix_ref, coef, heat, lefts)
+    rows = first_rows(DEEP_A, before_ref, 2 * NA, donor_ref, after_ref, 2 * NA)
+    run_members([(rows, (s0, s1), functools.partial(strided_store, donor))], coef, heat, lefts, DEEP_A)
+
+    def copy(m):
+        return pltpu.make_async_copy(donor, out_ref.at[m], sems.at[m])
+
+    for m in range(32):
+        @pl.when(killed_ref[m] > 0)
+        def _():
+            copy(m).start()
+
     zero = jnp.zeros((8, 128), jnp.float32)
     for k in range((NA + 7) // 8):
-        rows = [ref[pl.ds(16 * k + i, 8, stride=2), :] for ref in (before_ref, after_ref) for i in (0, 1)]
-        for slot, value in enumerate((rows[0], rows[1], rows[0], rows[2], rows[3], rows[2], zero, zero)):
+        parts = [ref[pl.ds(16 * k + i, 8, stride=2), :] for ref in (before_ref, after_ref) for i in (0, 1)]
+        for slot, value in enumerate((parts[0], parts[1], parts[0], parts[2], parts[3], parts[2], zero, zero)):
             edge[pl.ds(64 * k + slot, 8, stride=8), :] = value
-    score_members(NA, tq_ref, edge, land_ref, edge_mask(pup_ref, pdown_ref), weight_ref, head_ref, out_ref, 0)
-
-
-def score_b_kernel(tq_ref, edge_ref, pup_ref, pdown_ref, land_ref, weight_ref, head_ref, sums_ref, out_ref, acc):
-    acc[0:NA, :] = sums_ref[...]
-    score_members(NB, tq_ref, edge_ref, land_ref, edge_mask(pup_ref, pdown_ref), weight_ref, head_ref, acc, NA)
+    high, low = split(weight_ref[...])
+    left[...] = jnp.concatenate([high, low, high], 1)
+    land = land_ref[...].astype(jnp.float32)
+    mask = edge_mask(pup_ref, pdown_ref)
+    score_members(NA, tqa_ref, edge, land, mask, left, head_ref, acc, 0)
+    score_members(NB, tqb_ref, edgeb_ref, land, mask, left, head_ref, acc, NA)
     ones = jnp.ones((8, 128), jnp.float32)
     padded = jnp.concatenate([acc[...], jnp.zeros((96, 128), jnp.float32)], 0)
-    out_ref[...] = lax.dot_general(
+    sums = lax.dot_general(
         ones, padded, (((1,), (1,)), ((), ())), precision=lax.Precision.HIGHEST, preferred_element_type=jnp.float32
     )
+    for k in range(16):
+        sums_ref[pl.ds(8 * k, 8), :] = sums
+    for m in range(32):
+        @pl.when(killed_ref[m] > 0)
+        def _():
+            copy(m).wait()
 
 
 def weight_kernel(me_ref, parts_ref, counts_ref, source_ref, scores_ref, slot_ref):
@@ -395,16 +403,21 @@
     heat = heating.reshape(240, 128)
     hbm = pl.BlockSpec(memory_space=ANY)
 
-    def edge_scratch(count):
-        return [VMEM((count, 240, 128), jnp.float32), pltpu.SemaphoreType.DMA((count // BLK,))]
+    def edge_scratch(count, rows):
+        return [
+            VMEM((count, 240, 128), jnp.float32),
+            VMEM((rows, 128), jnp.float32),
+            VMEM((rows, 128), jnp.float32),
+            pltpu.SemaphoreType.DMA((3 * (count // BLK) + 2,)),
+        ]
 
     rows_a = NA * 120 + PARAMS
     pieces, send_up_a, send_down_a = call(
         edges_a_kernel,
         (f32(256, 128), f32(rows_a, 128), f32(rows_a, 128)),
         in_specs=[SCALAR, SCALAR, hbm, WHOLE, WHOLE, WHOLE],
-        out_specs=(WHOLE,) * 3,
-        scratch_shapes=edge_scratch(NA) + [pltpu.SemaphoreType.DMA],
+        out_specs=(WHOLE, hbm, hbm),
+        scratch_shapes=edge_scratch(NA, rows_a) + [pltpu.SemaphoreType.DMA],
         name="edges_a",
     )(me, counts, f, heat, diffusion, land_mask)
 
@@ -420,8 +433,8 @@
         edges_b_kernel,
         (f32(NB * 150, 128), f32(NB * 150, 128)),
         in_specs=[hbm],
-        out_specs=(WHOLE, WHOLE),
-        scratch_shapes=edge_scratch(NB),
+        out_specs=(hbm, hbm),
+        scratch_shapes=edge_scratch(NB, NB * 150),
         name="edges_b",
     )(f)
     up_b = lax.ppermute(send_up_b, "lat", up)
@@ -462,43 +475,41 @@
     before = lax.ppermute(send_up, "lat", up)
     after = lax.ppermute(send_down, "lat", down)
 
-    sums_a = call(
-        score_a_kernel,
-        f32(NA, 128),
-        grid=(1,),
-        in_specs=[WHOLE] * 3 + [params] * 2 + [WHOLE] * 3,
-        out_specs=WHOLE,
-        scratch_shapes=[VMEM(((NA + 7) // 8 * 64, 128), jnp.float32)],
-        name="score_a",
-    )(tq_a, before, after, up_a, down_a, land_mask, taps, head)
-
     halo_b = pl.BlockSpec((BLK * 30 * DEEP_B, 128), lambda i: (i, 0))
-    new_fields, tq_b, edge_b = call(
+    block_b = pl.BlockSpec((BLK, 240, 128), lambda i: (i + NA // BLK, 0, 0))
+    state_b, tq_b, edge_b = call(
         chunk_b_kernel,
         (f32(32, 240, 128), f32(NB, 16, 128), f32(NB, 8, 128)),
         grid=(NB // BLK,),
-        in_specs=[SCALAR, pl.BlockSpec((BLK, 240, 128), lambda i: (i + NA // BLK, 0, 0)), halo_b, halo_b]
-        + [WHOLE] * 3
-        + shared
-        + [hbm],
-        out_specs=(hbm, tq_block, pl.BlockSpec((BLK, 8, 128), lambda i: (i, 0, 0))),
-        scratch_shapes=step_scratch
-        + [VMEM((NB, 240, 128), jnp.float32), VMEM((240, 128), jnp.float32), pltpu.SemaphoreType.DMA((32,))],
-        input_output_aliases={12: 0},
+        in_specs=[block_b, halo_b, halo_b] + shared + [hbm],
+        out_specs=(block_b, tq_block, pl.BlockSpec((BLK, 8, 128), lambda i: (i, 0, 0))),
+        scratch_shapes=step_scratch,
+        input_output_aliases={8: 0},
         name="chunk_b",
-    )(killed, f, up_b, down_b, before, after, donor_state, up_a, down_a, heat, diffusion, mix, state_a)
-
-    partial = call(
-        score_b_kernel,
-        f32(8, 128),
+    )(f, up_b, down_b, up_a, down_a, heat, diffusion, mix, state_a)
+
+    new_fields, sums = call(
+        finish_kernel,
+        (f32(32, 240, 128), f32(128, 128)),
         grid=(1,),
-        in_specs=[WHOLE] * 2 + [params] * 2 + [WHOLE] * 4,
-        out_specs=WHOLE,
-        scratch_shapes=[VMEM((32, 128), jnp.float32)],
-        name="score_b",
-    )(tq_b, edge_b.reshape(NB * 8, 128), up_a, down_a, land_mask, taps, head, sums_a)
-
-    parts = lax.all_to_all(jnp.broadcast_to(partial[:1].reshape(1, 1, 128), (128, 1, 128)), ("lat", "grp"), 0, 0, tiled=True)
+        in_specs=[SCALAR] + [WHOLE] * 9 + shared + [hbm],
+        out_specs=(hbm, WHOLE),
+        scratch_shapes=step_scratch[:-2]
+        + [
+            VMEM((240, 128), jnp.float32),
+            VMEM(((NA + 7) // 8 * 64, 128), jnp.float32),
+            VMEM((256, 288), jnp.bfloat16),
+            VMEM((32, 128), jnp.float32),
+            pltpu.SemaphoreType.DMA((32,)),
+        ],
+        input_output_aliases={15: 0},
+        name="finish",
+    )(
+        killed, tq_a, before, after, tq_b, edge_b.reshape(NB * 8, 128), land_mask, taps, head, donor_state,
+        up_a, down_a, heat, diffusion, mix, state_b,
+    )
+
+    parts = lax.all_to_all(sums.reshape(128, 1, 128), ("lat", "grp"), 0, 0, tiled=True)
     scores, slot = call(
         weight_kernel, (f32(1, 32), f32(1, 32)), in_specs=[SCALAR] + [WHOLE] * 3, out_specs=(WHOLE, WHOLE), name="weights"
     )(me, parts.reshape(128, 128), counts2, source2)

time: 154 us -> 146 us (0.948)
  waiting for transfers between devices: 8.18 us -> 4.87 us
  Pallas kernels: 49.9 us -> 46.9 us
    ppermute x1, waiting for transfers between devices: 3.56 us -> 0.01 us  [local(): after = lax.ppermute(send_down, 'lat', down)]
    pallas_call x2 -> x1, Pallas kernels: 8.78 us -> 7.29 us  [local(): call(finish_kernel, (f32(32, 240, 128), f32(128, 128)), grid=(1,), in_spe...]
  transfers between devices with their start and end apart: 8 -> 8, of which waited for: 3 -> 2; matrix products, arithmetic and copies ran while one was open for 2% -> 2% of each run, Pallas kernels for 18% -> 23%
where the time goes in v1:
time: 146 us; the launch traced here: 145 us
  blocking collectives  57.2 us (39%)
  Pallas kernels  46.9 us (32%)
  starting transfers between devices  28.9 us (20%)
  waiting for transfers between devices  4.87 us (3%)
  local copies, waits for them, and re-layouts  4.41 us (3%)
  other arithmetic  1.83 us (1%)
    all_to_all x1, blocking collectives, local(): lax.all_to_all(sums.reshape(128, 1, 128), ('lat', 'grp'), 0, 0, tiled=True)  57.2 us
    pallas_call x1, Pallas kernels, local(): call(chunk_a_kernel, (f32(32, 240, 128), f32(NA, 16, 128)), grid=(NA // B...  16 us
    pallas_call x1, Pallas kernels, local(): call(chunk_b_kernel, (f32(32, 240, 128), f32(NB, 16, 128), f32(NB, 8, 128...  11.3 us
    all_to_all x1, starting transfers between devices, local(): lax.all_to_all(pieces.reshape(16, 16, 128), 'grp', 0, 0, tiled=True)  7.78 us
    pallas_call x1, Pallas kernels, local(): call(finish_kernel, (f32(32, 240, 128), f32(128, 128)), grid=(1,), in_spe...  7.29 us
    ppermute x1, starting transfers between devices, local(): up_b = lax.ppermute(send_up_b, 'lat', up)  4.93 us
    pallas_call x1, Pallas kernels, local(): call(edges_a_kernel, (f32(256, 128), f32(rows_a, 128), f32(rows_a, 128)),...  4.76 us
    ppermute x1, starting transfers between devices, local(): before = lax.ppermute(send_up, 'lat', up)  4.26 us
  transfers between devices with their start and end apart: 8, of which 2 were waited for; matrix products, arithmetic and copies ran while one was open for 2% of the time, Pallas kernels for 23%

profile of v1, /device:TPU:1, one launch (start us, length us, event | category | flops | bytes accessed | tf_op | source)
XLA Modules:
  0.0 145.1 jit_solution(3414340557865035552)
XLA Ops:
  0.6 0.0 copy-start
  0.7 0.0 copy-start.10
  0.7 0.0 copy-start.5
  0.7 0.0 copy-start.11
  0.7 0.0 copy-start.12
  0.7 4.8 %edges_a.1 = (f32[256,128]{1,0:T(8,128)}, f32[2560,128]{1,0:T(8,128)}, f32[2560,128]{1,0:T(8,128)}) custom-call(s32[1]{0:T(128)} %bitcast.2.me_ref, s32[512]{0:T(512)} %counts_ref.1, f32[32,240,128]{2,1,0:T(8,128)} %bitcast.21, f32[240,128]{1,0:T(8,128)} %bitcast.26, f32[8,128]{1,0:T(8,128)} %diff_ref.7, s32[8,128]{1,0:T(8,128)} %land_ref.3), custom_call_target="tpu_custom_call" | custom-call | tf_op jit(solution)/shard_map/edges_a/pallas_call | solution.py:415
  5.5 4.1 %collective-permute-start = (f32[2560,128]{1,0:T(8,128)}, f32[2560,128]{1,0:T(8,128)S(1)}, u32[]{:S(2)}, u32[]{:S(2)}) collective-permute-start(f32[2560,128]{1,0:T(8,128)} %get-tuple-element.19), channel_id=1, source_target_pairs={{0,16},{16,32},{32,48},{48,64},{64,80},{80,96},{96,112},{1,17},{17... | collective-permute-start | bytes 3932168 | tf_op jit(solution)/shard_map/ppermute | solution.py:425
  9.6 1.3 collective-permute-start.1
  10.9 2.5 %edges_b.1 = (f32[1800,128]{1,0:T(8,128)}, f32[1800,128]{1,0:T(8,128)}) custom-call(f32[32,240,128]{2,1,0:T(8,128)} %bitcast.22), custom_call_target="tpu_custom_call" | custom-call | tf_op jit(solution)/shard_map/edges_b/pallas_call | solution.py:432
  13.4 4.9 %collective-permute-start.4 = (f32[1800,128]{1,0:T(8,128)}, f32[1800,128]{1,0:T(8,128)}, u32[]{:S(2)}, u32[]{:S(2)}) collective-permute-start(f32[1800,128]{1,0:T(8,128)} %get-tuple-element.25), channel_id=1, source_target_pairs={{0,16},{16,32},{32,48},{48,64},{64,80},{80,96},{96,112},{1,17},{17... | collective-permute-start | bytes 2764808 | tf_op jit(solution)/shard_map/ppermute | solution.py:440
  18.3 1.3 collective-permute-start.5
  19.6 7.8 %all-to-all-start = ((f32[16,16,128]{2,1,0:T(8,128)}), f32[16,16,128]{2,1,0:T(8,128)S(1)}, u32[]{:S(2)}, u32[]{:S(2)}) async-start(f32[16,16,128]{2,1,0:T(8,128)} %bitcast.4), calls=%async_computation | async-start | bytes 262144 | tf_op jit(solution)/shard_map/all_to_all | solution.py:424
  27.4 0.0 copy-done.10
  27.4 0.0 copy-done
  27.4 0.0 copy-done.5
  27.5 0.2 convolution_bitcast_fusion
  27.7 0.0 copy-done.11
  27.7 0.1 reshape.65.counts_ref
  27.8 0.0 copy-done.12
  27.8 0.0 copy-start.9
  27.8 0.1 reshape.69.source_ref
  27.9 0.0 copy-start.8
  27.9 0.8 reshape.77.weight_ref
  28.6 0.1 pad.1.clone
  28.7 0.6 fusion.3.index_ref
  29.3 4.2 %all-to-all-done.pieces_ref = f32[16,16,128]{2,1,0:T(8,128)S(1)} async-done(((f32[16,16,128]{2,1,0:T(8,128)}), f32[16,16,128]{2,1,0:T(8,128)S(1)}, u32[]{:S(2)}, u32[]{:S(2)}) %all-to-all-start) | async-done | bytes 131104 | tf_op jit(solution)/shard_map/all_to_all | solution.py:424
  33.5 0.0 copy-start.4
  33.5 0.6 copy-done.4
  34.2 1.6 %pick.1 = f32[16,16,128]{2,1,0:T(8,128)} custom-call(s32[16]{0:T(128)} %fusion.3.index_ref, f32[16,16,128]{2,1,0:T(8,128)} %copy-done.4), custom_call_target="tpu_custom_call" | custom-call | tf_op jit(solution)/shard_map/pick/pallas_call | solution.py:429
  35.7 4.0 %all-to-all-start.1 = ((f32[16,16,128]{2,1,0:T(8,128)}), f32[16,16,128]{2,1,0:T(8,128)S(1)}, u32[]{:S(2)}, u32[]{:S(2)}) async-start(f32[16,16,128]{2,1,0:T(8,128)} %pick.1), calls=%async_computation.1 | async-start | bytes 262144 | tf_op jit(solution)/shard_map/all_to_all | solution.py:430
  39.7 0.7 fusion.mix_ref
  40.4 0.0 collective-permute-done.up_ref.pup_ref
  40.4 0.0 copy-start.1
  40.4 0.7 collective-permute-done.1.down_ref.pdown_ref
  41.1 0.4 copy-done.1
  41.4 0.0 copy-start.2
  41.4 1.1 copy-done.2
  42.5 16.0 %chunk_a.1 = (f32[32,240,128]{2,1,0:T(8,128)}, f32[20,16,128]{2,1,0:T(8,128)}) custom-call(f32[32,240,128]{2,1,0:T(8,128)} %bitcast.23, f32[2560,128]{1,0:T(8,128)} %copy-done.1, f32[2560,128]{1,0:T(8,128)} %copy-done.2, f32[2560,128]{1,0:T(8,128)} %copy-done.1, f32[2560,128]{1,0:T(8,128)} %copy-done.2, f32[240,128]{1,0:T(8,128)} %bitcast.27, ...), custom_call_target="tpu_custom_call" | custom-call | tf_op jit(solution)/shard_map/chunk_a/pallas_call | solution.py:462
  58.5 0.0 copy-done.8
  58.5 0.0 all-to-all-done.1
  58.5 0.0 copy-start.3
  58.5 0.6 copy-done.3
  59.1 1.7 %mid.1 = (f32[160,128]{1,0:T(8,128)}, f32[160,128]{1,0:T(8,128)}) custom-call(f32[256,128]{1,0:T(8,128)} %bitcast.30, f32[320,128]{1,0:T(8,128)} %bitcast.32), custom_call_target="tpu_custom_call" | custom-call | tf_op jit(solution)/shard_map/mid/pallas_call | solution.py:472
  60.8 4.3 %collective-permute-start.2 = (f32[160,128]{1,0:T(8,128)}, f32[160,128]{1,0:T(8,128)S(1)}, u32[]{:S(2)}, u32[]{:S(2)}) collective-permute-start(f32[160,128]{1,0:T(8,128)} %get-tuple-element.23), channel_id=1, source_target_pairs={{0,16},{16,32},{32,48},{48,64},{64,80},{80,96},{96,112},{1,17},{17... | collective-permute-start | bytes 245768 | tf_op jit(solution)/shard_map/ppermute | solution.py:475
  65.1 1.3 collective-permute-start.3
  66.4 0.0 copy-done.9
  66.4 0.5 fusion.5.killed_ref
  66.9 0.0 collective-permute-done.4.up_ref
  66.9 0.0 collective-permute-done.5.down_ref
  66.9 11.3 %chunk_b.1 = (f32[32,240,128]{2,1,0:T(8,128)}, f32[12,16,128]{2,1,0:T(8,128)}, f32[12,8,128]{2,1,0:T(8,128)}) custom-call(f32[32,240,128]{2,1,0:T(8,128)} %bitcast.24, f32[1800,128]{1,0:T(8,128)} %collective-permute-done.4.up_ref, f32[1800,128]{1,0:T(8,128)} %collective-permute-done.5.down_ref, ...), custom_call_target="tpu_custom_call", output_to_operand_aliasing={{0}: (8, {})} | custom-call | tf_op jit(solution)/shard_map/chunk_b/pallas_call | solution.py:480
  78.3 0.0 collective-permute-done.2.before_ref
  78.3 0.0 copy-start.6
  78.3 0.0 collective-permute-done.3.after_ref
  78.3 0.0 copy-start.7
  78.3 0.6 copy-done.6
  78.9 0.1 copy-done.7
  79.0 7.3 %finish.1 = (f32[32,240,128]{2,1,0:T(8,128)}, f32[128,128]{1,0:T(8,128)}) custom-call(s32[32]{0:T(128)} %fusion.5.killed_ref, f32[20,16,128]{2,1,0:T(8,128)} %get-tuple-element.21.tqa_ref, f32[160,128]{1,0:T(8,128)} %copy-done.6, f32[160,128]{1,0:T(8,128)} %copy-done.7, f32[12,16,128]{2,1,0:T(8,128)} %get-tuple-element.28.tqb_ref, ...), custom_call_target="tpu_custom_call", output_to_operand_aliasing={{0}: (15, {})} | custom-call | tf_op jit(solution)/shard_map/finish/pallas_call | solution.py:491
  86.3 57.2 %all_to_all.15 = f32[128,1,128]{2,1,0:T(1,128)} all-to-all(f32[128,1,128]{2,1,0:T(1,128)} %bitcast.35), channel_id=1, replica_groups=mesh['lat'=8,'grp'=16] {'lat','grp'}, dimensions={0} | all-to-all | bytes 131072 | tf_op jit(solution)/shard_map/all_to_all | solution.py:512
  143.4 1.7 %weights.1 = (f32[1,32]{1,0:T(1,128)}, f32[1,32]{1,0:T(1,128)}) custom-call(s32[1]{0:T(128)} %bitcast.2.me_ref, f32[128,128]{1,0:T(8,128)} %bitcast.33, s32[16,32]{1,0:T(8,128)} %copy-done.9, s32[16,32]{1,0:T(8,128)} %copy-done.8), custom_call_target="tpu_custom_call" | custom-call | tf_op jit(solution)/shard_map/weights/pallas_call | solution.py:513
  (4 shorter events, 0.0 us)
Async XLA Ops:
  0.6 26.8 %copy-start = (f32[32,27]{1,0:T(8,128)S(1)}, f32[32,27]{1,0:T(8,128)}, u32[]{:S(2)}) copy-start(f32[32,27]{1,0:T(8,128)} %param.15) | copy-start | bytes 10372
  0.7 26.8 %copy-start.10 = (f32[30,30]{1,0:T(8,128)S(1)}, f32[30,30]{1,0:T(8,128)}, u32[]{:S(2)}) copy-start(f32[30,30]{1,0:T(8,128)} %param.12) | copy-start | bytes 10804
  0.7 26.8 %copy-start.5 = (f32[27,768]{1,0:T(8,128)S(1)}, f32[27,768]{1,0:T(8,128)}, u32[]{:S(2)}) copy-start(f32[27,768]{1,0:T(8,128)} %constant.35.clone) | copy-start | bytes 248836
  0.7 27.0 %copy-start.11 = (s32[512]{0:T(512)S(1)}, s32[512]{0:T(512)}, u32[]{:S(2)}) copy-start(s32[512]{0:T(512)} %counts_ref.1) | copy-start | bytes 6148
  0.7 27.1 %copy-start.12 = (s32[512]{0:T(512)S(1)}, s32[512]{0:T(512)}, u32[]{:S(2)}) copy-start(s32[512]{0:T(512)} %param.18) | copy-start | bytes 6148
  5.5 34.9 %collective-permute-start = (f32[2560,128]{1,0:T(8,128)}, f32[2560,128]{1,0:T(8,128)S(1)}, u32[]{:S(2)}, u32[]{:S(2)}) collective-permute-start(f32[2560,128]{1,0:T(8,128)} %get-tuple-element.19), channel_id=1, source_target_pairs={{0,16},{16,32},{32,48},{48,64},{64,80},{80,96},{96,112},{1,17},{17... | collective-permute-start | bytes 3932168 | tf_op jit(solution)/shard_map/ppermute | solution.py:425
  9.6 31.5 %collective-permute-start.1 = (f32[2560,128]{1,0:T(8,128)}, f32[2560,128]{1,0:T(8,128)S(1)}, u32[]{:S(2)}, u32[]{:S(2)}) collective-permute-start(f32[2560,128]{1,0:T(8,128)} %get-tuple-element.20), channel_id=1, source_target_pairs={{16,0},{32,16},{48,32},{64,48},{80,64},{96,80},{112,96},{17,1},{33... | collective-permute-start | bytes 3932168 | tf_op jit(solution)/shard_map/ppermute | solution.py:426
  13.4 53.5 %collective-permute-start.4 = (f32[1800,128]{1,0:T(8,128)}, f32[1800,128]{1,0:T(8,128)}, u32[]{:S(2)}, u32[]{:S(2)}) collective-permute-start(f32[1800,128]{1,0:T(8,128)} %get-tuple-element.25), channel_id=1, source_target_pairs={{0,16},{16,32},{32,48},{48,64},{64,80},{80,96},{96,112},{1,17},{17... | collective-permute-start | bytes 2764808 | tf_op jit(solution)/shard_map/ppermute | solution.py:440
  18.3 48.6 %collective-permute-start.5 = (f32[1800,128]{1,0:T(8,128)}, f32[1800,128]{1,0:T(8,128)}, u32[]{:S(2)}, u32[]{:S(2)}) collective-permute-start(f32[1800,128]{1,0:T(8,128)} %get-tuple-element.26), channel_id=1, source_target_pairs={{16,0},{32,16},{48,32},{64,48},{80,64},{96,80},{112,96},{17,1},{33... | collective-permute-start | bytes 2764808 | tf_op jit(solution)/shard_map/ppermute | solution.py:441
  19.6 13.9 %all-to-all-start = ((f32[16,16,128]{2,1,0:T(8,128)}), f32[16,16,128]{2,1,0:T(8,128)S(1)}, u32[]{:S(2)}, u32[]{:S(2)}) async-start(f32[16,16,128]{2,1,0:T(8,128)} %bitcast.4), calls=%async_computation | async-start | bytes 262144 | tf_op jit(solution)/shard_map/all_to_all | solution.py:424
  27.8 38.6 %copy-start.9 = (s32[16,32]{1,0:T(8,128)}, s32[16,32]{1,0:T(8,128)S(1)}, u32[]{:S(2)}) copy-start(s32[16,32]{1,0:T(8,128)S(1)} %reshape.65.counts_ref) | copy-start | bytes 6148
  27.9 30.6 %copy-start.8 = (s32[16,32]{1,0:T(8,128)}, s32[16,32]{1,0:T(8,128)S(1)}, u32[]{:S(2)}) copy-start(s32[16,32]{1,0:T(8,128)S(1)} %reshape.69.source_ref) | copy-start | bytes 6148
  33.5 0.6 copy-start.4
  35.7 22.7 %all-to-all-start.1 = ((f32[16,16,128]{2,1,0:T(8,128)}), f32[16,16,128]{2,1,0:T(8,128)S(1)}, u32[]{:S(2)}, u32[]{:S(2)}) async-start(f32[16,16,128]{2,1,0:T(8,128)} %pick.1), calls=%async_computation.1 | async-start | bytes 262144 | tf_op jit(solution)/shard_map/all_to_all | solution.py:430
  40.4 1.1 copy-start.1
  41.4 1.1 copy-start.2
  58.5 0.7 copy-start.3
  60.8 17.4 %collective-permute-start.2 = (f32[160,128]{1,0:T(8,128)}, f32[160,128]{1,0:T(8,128)S(1)}, u32[]{:S(2)}, u32[]{:S(2)}) collective-permute-start(f32[160,128]{1,0:T(8,128)} %get-tuple-element.23), channel_id=1, source_target_pairs={{0,16},{16,32},{32,48},{48,64},{64,80},{80,96},{96,112},{1,17},{17... | collective-permute-start | bytes 245768 | tf_op jit(solution)/shard_map/ppermute | solution.py:475
  65.1 13.2 %collective-permute-start.3 = (f32[160,128]{1,0:T(8,128)}, f32[160,128]{1,0:T(8,128)S(1)}, u32[]{:S(2)}, u32[]{:S(2)}) collective-permute-start(f32[160,128]{1,0:T(8,128)} %get-tuple-element.24), channel_id=1, source_target_pairs={{16,0},{32,16},{48,32},{64,48},{80,64},{96,80},{112,96},{17,1},{33... | collective-permute-start | bytes 245768 | tf_op jit(solution)/shard_map/ppermute | solution.py:476
  78.3 0.6 copy-start.6
  78.3 0.7 copy-start.7

commit v2 on v1

--- a/solution.py
+++ b/solution.py
@@ -127,11 +127,14 @@
 
 
 def chunk_a_kernel(
-    f_ref, up_ref, down_ref, pup_ref, pdown_ref, hown_ref, diff_ref, mix_ref, out_ref, tq_ref, coef, heat, lefts, *states
+    f_ref, up_ref, down_ref, pup_ref, pdown_ref, hown_ref, diff_ref, mix_ref, out_ref, tq_ref, pup_out, pdown_out, coef, heat, lefts,
+    *states,
 ):
     @pl.when(pl.program_id(0) == 0)
     def _():
         prepare(pup_ref, pdown_ref, hown_ref, diff_ref, mix_ref, coef, heat, lefts)
+        pup_out[...] = pup_ref[...]
+        pdown_out[...] = pdown_ref[...]
 
     def one(p, carry):
         members = []
@@ -224,15 +227,18 @@
 
 
 def edges_a_kernel(
-    me_ref, counts_ref, f_ref, heat_ref, diff_ref, land_ref, pieces_ref, up_ref, down_ref, buf, up_buf, down_buf, sems, hot_sem
+    me_ref, counts_ref, f_ref, heat_ref, diff_ref, land_ref, pieces_ref, up_ref, down_ref, buf, up_buf, down_buf, sems, pieces, hot_sems
 ):
-    me = me_ref[0]
-    hot = lax.fori_loop(0, 32, lambda j, at: jnp.where(counts_ref[me * 32 + j] >= 2, j, at), 0)
-    fetch = pltpu.make_async_copy(f_ref.at[hot], pieces_ref.at[pl.ds(0, 240)], hot_sem)
-    fetch.start()
+    put_pieces = pltpu.make_async_copy(pieces, pieces_ref, hot_sems.at[1])
 
     def before():
-        pieces_ref[240:256, :] = jnp.zeros((16, 128), jnp.float32)
+        base = me_ref[0] * 32
+        hot = jnp.int32(0)
+        for j in range(1, 32):
+            hot = jnp.where(counts_ref[base + j] >= 2, j, hot)
+        fetch = pltpu.make_async_copy(f_ref.at[hot], pieces.at[pl.ds(0, 240)], hot_sems.at[0])
+        fetch.start()
+        pieces[240:256, :] = jnp.zeros((16, 128), jnp.float32)
         base = NA * 120
         send_rows(heat_ref, up_buf, down_buf, base, 5)
         diff = diff_ref[...]
@@ -241,10 +247,12 @@
         up_buf[base + 155 : base + 160, :] = land[3:]
         down_buf[base + 150 : base + 155, :] = diff[:5]
         down_buf[base + 155 : base + 160, :] = land[:5]
+        fetch.wait()
+        put_pieces.start()
         return PARAMS
 
     send_members(f_ref, 0, NA, DEEP_A, up_ref, down_ref, buf, up_buf, down_buf, sems, before)
-    fetch.wait()
+    put_pieces.wait()
 
 
 def edges_b_kernel(f_ref, up_ref, down_ref, buf, up_buf, down_buf, sems):
@@ -384,8 +392,12 @@
     return table.reshape(27, 8 * 96)
 
 
-def call(kernel, outs, **kw):
-    return pl.pallas_call(kernel, out_shape=outs, **kw)
+GRANT = {"chunk_a": 50, "chunk_b": 53, "pick": 24, "mid": 24, "finish": 24, "weights": 24}
+
+
+def call(kernel, outs, name, **kw):
+    params = pltpu.CompilerParams(vmem_limit_bytes=GRANT[name] << 20) if name in GRANT else None
+    return pl.pallas_call(kernel, out_shape=outs, compiler_params=params, **kw)
 
 
 def f32(*shape):
@@ -416,8 +428,8 @@
         edges_a_kernel,
         (f32(256, 128), f32(rows_a, 128), f32(rows_a, 128)),
         in_specs=[SCALAR, SCALAR, hbm, WHOLE, WHOLE, WHOLE],
-        out_specs=(WHOLE, hbm, hbm),
-        scratch_shapes=edge_scratch(NA, rows_a) + [pltpu.SemaphoreType.DMA],
+        out_specs=(hbm, hbm, hbm),
+        scratch_shapes=edge_scratch(NA, rows_a) + [VMEM((256, 128), jnp.float32), pltpu.SemaphoreType.DMA((2,))],
         name="edges_a",
     )(me, counts, f, heat, diffusion, land_mask)
 
@@ -459,12 +471,13 @@
     ] + [VMEM((18 * 32, 128), jnp.float32)] * 4
     shared = [params, params, WHOLE, WHOLE, WHOLE]
     halo_a = pl.BlockSpec((BLK * 30 * DEEP_A, 128), lambda i: (i, 0))
-    state_a, tq_a = call(
+    whole_params = whole((PARAMS, 128))
+    state_a, tq_a, params_up, params_down = call(
         chunk_a_kernel,
-        (f32(32, 240, 128), f32(NA, 16, 128)),
+        (f32(32, 240, 128), f32(NA, 16, 128), f32(PARAMS, 128), f32(PARAMS, 128)),
         grid=(NA // BLK,),
         in_specs=[block, halo_a, halo_a] + shared,
-        out_specs=(block, tq_block),
+        out_specs=(block, tq_block, whole_params, whole_params),
         scratch_shapes=step_scratch,
         name="chunk_a",
     )(f, up_a, down_a, up_a, down_a, heat, diffusion, mix)
@@ -481,18 +494,18 @@
         chunk_b_kernel,
         (f32(32, 240, 128), f32(NB, 16, 128), f32(NB, 8, 128)),
         grid=(NB // BLK,),
-        in_specs=[block_b, halo_b, halo_b] + shared + [hbm],
+        in_specs=[block_b, halo_b, halo_b] + [WHOLE] * 5 + [hbm],
         out_specs=(block_b, tq_block, pl.BlockSpec((BLK, 8, 128), lambda i: (i, 0, 0))),
         scratch_shapes=step_scratch,
         input_output_aliases={8: 0},
         name="chunk_b",
-    )(f, up_b, down_b, up_a, down_a, heat, diffusion, mix, state_a)
+    )(f, up_b, down_b, params_up, params_down, heat, diffusion, mix, state_a)
 
     new_fields, sums = call(
         finish_kernel,
         (f32(32, 240, 128), f32(128, 128)),
         grid=(1,),
-        in_specs=[SCALAR] + [WHOLE] * 9 + shared + [hbm],
+        in_specs=[SCALAR] + [WHOLE] * 14 + [hbm],
         out_specs=(hbm, WHOLE),
         scratch_shapes=step_scratch[:-2]
         + [
@@ -506,7 +519,7 @@
         name="finish",
     )(
         killed, tq_a, before, after, tq_b, edge_b.reshape(NB * 8, 128), land_mask, taps, head, donor_state,
-        up_a, down_a, heat, diffusion, mix, state_b,
+        params_up, params_down, heat, diffusion, mix, state_b,
     )
 
     parts = lax.all_to_all(sums.reshape(128, 1, 128), ("lat", "grp"), 0, 0, tiled=True)

time: 146 us -> 135 us (0.925)
  Pallas kernels: 46.9 us -> 41.5 us
  local copies, waits for them, and re-layouts: 4.41 us -> 0.39 us
  waiting for transfers between devices: 4.87 us -> 7.69 us
  blocking collectives: 57.2 us -> 55.5 us
  other arithmetic: 1.83 us -> 0.22 us
    unnamed x26 -> x18, local copies, waits for them, and re-layouts: 3.41 us -> 0.05 us
    all_to_all x1, blocking collectives: 57.2 us -> 55.5 us  [local(): lax.all_to_all(sums.reshape(128, 1, 128), ('lat', 'grp'), 0, 0, tiled=True)]
    ppermute x1, waiting for transfers between devices: 0.69 us -> 2.35 us  [local(): down_a = lax.ppermute(send_down_a, 'lat', down)]
    pallas_call x1, Pallas kernels: 1.68 us -> 0.03 us  [local(): call(mid_kernel, (f32(MID, 128), f32(MID, 128)), in_specs=[WHOLE, WHOLE],...]
  transfers between devices with their start and end apart: 8 -> 8, of which waited for: 2 -> 2; matrix products, arithmetic and copies ran while one was open for 2% -> 1% of each run, Pallas kernels for 23% -> 23%
where the time goes in v2:
time: 135 us; the launch traced here: 134 us
  blocking collectives  55.5 us (41%)
  Pallas kernels  41.5 us (31%)
  starting transfers between devices  27.9 us (21%)
  waiting for transfers between devices  7.69 us (6%)
    all_to_all x1, blocking collectives, local(): lax.all_to_all(sums.reshape(128, 1, 128), ('lat', 'grp'), 0, 0, tiled=True)  55.5 us
    pallas_call x1, Pallas kernels, local(): call(chunk_a_kernel, (f32(32, 240, 128), f32(NA, 16, 128), f32(PARAMS, 12...  15.6 us
    pallas_call x1, Pallas kernels, local(): call(chunk_b_kernel, (f32(32, 240, 128), f32(NB, 16, 128), f32(NB, 8, 128...  11.1 us
    all_to_all x1, starting transfers between devices, local(): lax.all_to_all(pieces.reshape(16, 16, 128), 'grp', 0, 0, tiled=True)  7.78 us
    pallas_call x1, Pallas kernels, local(): call(finish_kernel, (f32(32, 240, 128), f32(128, 128)), grid=(1,), in_spe...  5.88 us
    all_to_all x1, waiting for transfers between devices, local(): lax.all_to_all(pieces.reshape(16, 16, 128), 'grp', 0, 0, tiled=True)  5.32 us
    ppermute x1, starting transfers between devices, local(): up_b = lax.ppermute(send_up_b, 'lat', up)  4.94 us
    pallas_call x1, Pallas kernels, local(): call(edges_a_kernel, (f32(256, 128), f32(rows_a, 128), f32(rows_a, 128)),...  4.37 us
  transfers between devices with their start and end apart: 8, of which 2 were waited for; matrix products, arithmetic and copies ran while one was open for 1% of the time, Pallas kernels for 23%

profile of v2, /device:TPU:1, one launch (start us, length us, event | category | flops | bytes accessed | tf_op | source)
XLA Modules:
  0.0 134.3 jit_solution(18394956763910500134)
XLA Ops:
  0.6 0.0 copy-start
  0.7 0.0 copy-start.6
  0.7 0.0 copy-start.5
  0.7 0.0 copy-start.7
  0.7 0.0 copy-start.8
  0.7 0.0 copy-start.1
  0.7 0.0 copy-start.3
  0.7 4.4 %shard_map.121 = (f32[256,128]{1,0:T(8,128)}, f32[2560,128]{1,0:T(8,128)}, f32[2560,128]{1,0:T(8,128)}) custom-call(s32[1]{0:T(128)} %bitcast.2.me_ref, s32[512]{0:T(512)} %counts_ref.1, f32[32,240,128]{2,1,0:T(8,128)} %bitcast.32, f32[240,128]{1,0:T(8,128)} %bitcast.21, f32[8,128]{1,0:T(8,128)} %diff_ref.7, s32[8,128]{1,0:T(8,128)} %land_ref.3), custom_call_target="tpu_custom_call" | custom-call | tf_op jit(solution)/shard_map/pallas_call | solution.py:427
  5.1 4.1 %collective-permute-start = (f32[2560,128]{1,0:T(8,128)}, f32[2560,128]{1,0:T(8,128)S(1)}, u32[]{:S(2)}, u32[]{:S(2)}) collective-permute-start(f32[2560,128]{1,0:T(8,128)} %get-tuple-element.21), channel_id=1, source_target_pairs={{0,16},{16,32},{32,48},{48,64},{64,80},{80,96},{96,112},{1,17},{17... | collective-permute-start | bytes 3932168 | tf_op jit(solution)/shard_map/ppermute | solution.py:437
  9.2 1.3 collective-permute-start.1
  10.5 2.5 %shard_map.125 = (f32[1800,128]{1,0:T(8,128)}, f32[1800,128]{1,0:T(8,128)}) custom-call(f32[32,240,128]{2,1,0:T(8,128)} %bitcast.33), custom_call_target="tpu_custom_call" | custom-call | tf_op jit(solution)/shard_map/pallas_call | solution.py:444
  13.0 4.9 %collective-permute-start.4 = (f32[1800,128]{1,0:T(8,128)}, f32[1800,128]{1,0:T(8,128)}, u32[]{:S(2)}, u32[]{:S(2)}) collective-permute-start(f32[1800,128]{1,0:T(8,128)} %get-tuple-element.27), channel_id=1, source_target_pairs={{0,16},{16,32},{32,48},{48,64},{64,80},{80,96},{96,112},{1,17},{17... | collective-permute-start | bytes 2764808 | tf_op jit(solution)/shard_map/ppermute | solution.py:452
  17.9 1.3 collective-permute-start.5
  19.2 7.8 %all-to-all-start = ((f32[16,16,128]{2,1,0:T(8,128)}), f32[16,16,128]{2,1,0:T(8,128)S(1)}, u32[]{:S(2)}, u32[]{:S(2)}) async-start(f32[16,16,128]{2,1,0:T(8,128)} %bitcast.4), calls=%async_computation | async-start | bytes 262144 | tf_op jit(solution)/shard_map/all_to_all | solution.py:436
  27.0 0.0 copy-done.6
  27.0 0.0 copy-done
  27.0 0.0 copy-done.5
  27.0 0.2 convolution_bitcast_fusion
  27.3 0.0 copy-done.7
  27.3 0.1 reshape.65.counts_ref
  27.4 0.0 copy-done.8
  27.4 0.1 reshape.69.source_ref
  27.5 0.1 reshape.77.weight_ref
  27.6 0.1 pad.1.clone
  27.7 0.1 fusion.3.index_ref
  27.8 5.3 %all-to-all-done.pieces_ref = f32[16,16,128]{2,1,0:T(8,128)S(1)} async-done(((f32[16,16,128]{2,1,0:T(8,128)}), f32[16,16,128]{2,1,0:T(8,128)S(1)}, u32[]{:S(2)}, u32[]{:S(2)}) %all-to-all-start) | async-done | bytes 131104 | tf_op jit(solution)/shard_map/all_to_all | solution.py:436
  33.1 1.2 shard_map.123
  34.3 4.0 %all-to-all-start.1 = ((f32[16,16,128]{2,1,0:T(8,128)}), f32[16,16,128]{2,1,0:T(8,128)S(1)}, u32[]{:S(2)}, u32[]{:S(2)}) async-start(f32[16,16,128]{2,1,0:T(8,128)} %shard_map.123), calls=%async_computation.1 | async-start | bytes 262144 | tf_op jit(solution)/shard_map/all_to_all | solution.py:442
  38.3 0.1 fusion.mix_ref
  38.3 0.0 collective-permute-done.up_ref.pup_ref
  38.3 2.4 %collective-permute-done.1.down_ref.pdown_ref = f32[2560,128]{1,0:T(8,128)S(1)} collective-permute-done((f32[2560,128]{1,0:T(8,128)}, f32[2560,128]{1,0:T(8,128)S(1)}, u32[]{:S(2)}, u32[]{:S(2)}) %collective-permute-start.1) | collective-permute-done | bytes 1310752 | tf_op jit(solution)/shard_map/ppermute | solution.py:438
  40.7 0.0 copy-done.1
  40.7 0.0 copy-done.3
  40.7 15.6 %shard_map.122 = (f32[32,240,128]{2,1,0:T(8,128)}, f32[20,16,128]{2,1,0:T(8,128)S(1)}, f32[160,128]{1,0:T(8,128)S(1)}, f32[160,128]{1,0:T(8,128)S(1)}) custom-call(f32[32,240,128]{2,1,0:T(8,128)} %bitcast.34, f32[2560,128]{1,0:T(8,128)S(1)} %collective-permute-done.up_ref.pup_ref, f32[2560,128]{1,0:T(8,128)S(1)} %collective-permute-done.1.down_ref.pdown_ref, ...), custom_call_target="tpu_custom_call" | custom-call | tf_op jit(solution)/shard_map/pallas_call | solution.py:475
  56.3 0.0 all-to-all-done.1
  56.3 3.2 %collective-permute-start.2 = (f32[160,128]{1,0:T(8,128)S(1)}, f32[160,128]{1,0:T(8,128)S(1)}, u32[]{:S(2)}, u32[]{:S(2)}) collective-permute-start(f32[160,128]{1,0:T(8,128)S(1)} %get-tuple-element.25), channel_id=1, source_target_pairs={{0,16},{16,32},{32,48},{48,64},{64,80},{80,96},{96,112},{1,17},{17... | collective-permute-start | bytes 245768 | tf_op jit(solution)/shard_map/ppermute | solution.py:488
  59.5 1.3 collective-permute-start.3
  60.9 0.0 collective-permute-done.4.up_ref
  60.9 0.0 collective-permute-done.5.down_ref
  60.9 0.0 copy-start.2
  60.9 0.0 copy-start.4
  60.9 11.1 %shard_map.126 = (f32[32,240,128]{2,1,0:T(8,128)}, f32[12,16,128]{2,1,0:T(8,128)S(1)}, f32[12,8,128]{2,1,0:T(8,128)S(1)}) custom-call(f32[32,240,128]{2,1,0:T(8,128)} %bitcast.35, f32[1800,128]{1,0:T(8,128)} %collective-permute-done.4.up_ref, f32[1800,128]{1,0:T(8,128)} %collective-permute-done.5.down_ref, ...), custom_call_target="tpu_custom_call", output_to_operand_aliasing={{0}: (8, {})} | custom-call | tf_op jit(solution)/shard_map/pallas_call | solution.py:493
  72.0 0.0 collective-permute-done.2.before_ref
  72.0 0.0 collective-permute-done.3.after_ref
  72.0 0.0 copy-done.2
  72.1 0.0 copy-done.4
  72.1 5.9 %shard_map.127 = (f32[32,240,128]{2,1,0:T(8,128)}, f32[128,128]{1,0:T(8,128)S(1)}) custom-call(s32[32]{0:T(128)S(1)} %fusion.5.killed_ref, f32[20,16,128]{2,1,0:T(8,128)S(1)} %get-tuple-element.23.tqa_ref, f32[160,128]{1,0:T(8,128)S(1)} %collective-permute-done.2.before_ref, ...), custom_call_target="tpu_custom_call", output_to_operand_aliasing={{0}: (15, {})} | custom-call | tf_op jit(solution)/shard_map/pallas_call | solution.py:504
  78.0 55.5 %all_to_all.15 = f32[128,1,128]{2,1,0:T(1,128)S(1)} all-to-all(f32[128,1,128]{2,1,0:T(1,128)S(1)} %bitcast.30), channel_id=1, replica_groups=mesh['lat'=8,'grp'=16] {'lat','grp'}, dimensions={0} | all-to-all | bytes 131072 | tf_op jit(solution)/shard_map/all_to_all | solution.py:525
  133.4 0.8 shard_map.128
  (6 shorter events, 0.1 us)
Async XLA Ops:
  0.6 26.4 %copy-start = (f32[32,27]{1,0:T(8,128)S(1)}, f32[32,27]{1,0:T(8,128)}, u32[]{:S(2)}) copy-start(f32[32,27]{1,0:T(8,128)} %param.15) | copy-start | bytes 10372
  0.7 26.3 %copy-start.6 = (f32[30,30]{1,0:T(8,128)S(1)}, f32[30,30]{1,0:T(8,128)}, u32[]{:S(2)}) copy-start(f32[30,30]{1,0:T(8,128)} %param.12) | copy-start | bytes 10804
  0.7 26.4 %copy-start.5 = (f32[27,768]{1,0:T(8,128)S(1)}, f32[27,768]{1,0:T(8,128)}, u32[]{:S(2)}) copy-start(f32[27,768]{1,0:T(8,128)} %constant.35.clone) | copy-start | bytes 248836
  0.7 26.6 %copy-start.7 = (s32[512]{0:T(512)S(1)}, s32[512]{0:T(512)}, u32[]{:S(2)}) copy-start(s32[512]{0:T(512)} %counts_ref.1) | copy-start | bytes 6148
  0.7 26.7 %copy-start.8 = (s32[512]{0:T(512)S(1)}, s32[512]{0:T(512)}, u32[]{:S(2)}) copy-start(s32[512]{0:T(512)} %param.18) | copy-start | bytes 6148
  0.7 40.0 %copy-start.1 = (f32[30,8,128]{2,1,0:T(8,128)S(1)}, f32[30,8,128]{2,1,0:T(8,128)}, u32[]{:S(2)}) copy-start(f32[30,8,128]{2,1,0:T(8,128)} %param.13) | copy-start | bytes 368644
  0.7 40.0 %copy-start.3 = (f32[8,128]{1,0:T(8,128)S(1)}, f32[8,128]{1,0:T(8,128)}, u32[]{:S(2)}) copy-start(f32[8,128]{1,0:T(8,128)} %diff_ref.7) | copy-start | bytes 12292
  5.1 33.2 %collective-permute-start = (f32[2560,128]{1,0:T(8,128)}, f32[2560,128]{1,0:T(8,128)S(1)}, u32[]{:S(2)}, u32[]{:S(2)}) collective-permute-start(f32[2560,128]{1,0:T(8,128)} %get-tuple-element.21), channel_id=1, source_target_pairs={{0,16},{16,32},{32,48},{48,64},{64,80},{80,96},{96,112},{1,17},{17... | collective-permute-start | bytes 3932168 | tf_op jit(solution)/shard_map/ppermute | solution.py:437
  9.2 31.5 %collective-permute-start.1 = (f32[2560,128]{1,0:T(8,128)}, f32[2560,128]{1,0:T(8,128)S(1)}, u32[]{:S(2)}, u32[]{:S(2)}) collective-permute-start(f32[2560,128]{1,0:T(8,128)} %get-tuple-element.22), channel_id=1, source_target_pairs={{16,0},{32,16},{48,32},{64,48},{80,64},{96,80},{112,96},{17,1},{33... | collective-permute-start | bytes 3932168 | tf_op jit(solution)/shard_map/ppermute | solution.py:438
  13.0 47.9 %collective-permute-start.4 = (f32[1800,128]{1,0:T(8,128)}, f32[1800,128]{1,0:T(8,128)}, u32[]{:S(2)}, u32[]{:S(2)}) collective-permute-start(f32[1800,128]{1,0:T(8,128)} %get-tuple-element.27), channel_id=1, source_target_pairs={{0,16},{16,32},{32,48},{48,64},{64,80},{80,96},{96,112},{1,17},{17... | collective-permute-start | bytes 2764808 | tf_op jit(solution)/shard_map/ppermute | solution.py:452
  17.9 43.0 %collective-permute-start.5 = (f32[1800,128]{1,0:T(8,128)}, f32[1800,128]{1,0:T(8,128)}, u32[]{:S(2)}, u32[]{:S(2)}) collective-permute-start(f32[1800,128]{1,0:T(8,128)} %get-tuple-element.28), channel_id=1, source_target_pairs={{16,0},{32,16},{48,32},{64,48},{80,64},{96,80},{112,96},{17,1},{33... | collective-permute-start | bytes 2764808 | tf_op jit(solution)/shard_map/ppermute | solution.py:453
  19.2 13.9 %all-to-all-start = ((f32[16,16,128]{2,1,0:T(8,128)}), f32[16,16,128]{2,1,0:T(8,128)S(1)}, u32[]{:S(2)}, u32[]{:S(2)}) async-start(f32[16,16,128]{2,1,0:T(8,128)} %bitcast.4), calls=%async_computation | async-start | bytes 262144 | tf_op jit(solution)/shard_map/all_to_all | solution.py:436
  34.3 22.0 %all-to-all-start.1 = ((f32[16,16,128]{2,1,0:T(8,128)}), f32[16,16,128]{2,1,0:T(8,128)S(1)}, u32[]{:S(2)}, u32[]{:S(2)}) async-start(f32[16,16,128]{2,1,0:T(8,128)} %shard_map.123), calls=%async_computation.1 | async-start | bytes 262144 | tf_op jit(solution)/shard_map/all_to_all | solution.py:442
  56.3 15.7 %collective-permute-start.2 = (f32[160,128]{1,0:T(8,128)S(1)}, f32[160,128]{1,0:T(8,128)S(1)}, u32[]{:S(2)}, u32[]{:S(2)}) collective-permute-start(f32[160,128]{1,0:T(8,128)S(1)} %get-tuple-element.25), channel_id=1, source_target_pairs={{0,16},{16,32},{32,48},{48,64},{64,80},{80,96},{96,112},{1,17},{17... | collective-permute-start | bytes 245768 | tf_op jit(solution)/shard_map/ppermute | solution.py:488
  59.5 12.5 %collective-permute-start.3 = (f32[160,128]{1,0:T(8,128)S(1)}, f32[160,128]{1,0:T(8,128)S(1)}, u32[]{:S(2)}, u32[]{:S(2)}) collective-permute-start(f32[160,128]{1,0:T(8,128)S(1)} %get-tuple-element.26), channel_id=1, source_target_pairs={{16,0},{32,16},{48,32},{64,48},{80,64},{96,80},{112,96},{17,1},{33... | collective-permute-start | bytes 245768 | tf_op jit(solution)/shard_map/ppermute | solution.py:489
  60.9 11.2 %copy-start.2 = (f32[32,8,128]{2,1,0:T(8,128)S(1)}, f32[32,8,128]{2,1,0:T(8,128)}, u32[]{:S(2)}) copy-start(f32[32,8,128]{2,1,0:T(8,128)} %param.16) | copy-start | bytes 393220
  60.9 11.2 %copy-start.4 = (s32[8,128]{1,0:T(8,128)S(1)}, s32[8,128]{1,0:T(8,128)}, u32[]{:S(2)}) copy-start(s32[8,128]{1,0:T(8,128)} %land_ref.3) | copy-start | bytes 12292

commit v3 on v2

--- a/solution.py
+++ b/solution.py
@@ -56,51 +56,93 @@
     return first_row
 
 
+INNER = {(1, 1): 0, (1, 2): 1, (1, 5): 2, (1, 6): 3, (2, 2): 4, (2, 3): 5, (2, 4): 6, (2, 5): 7, (3, 3): 8, (3, 4): 9}
+INNER_PAIRS = {1: [(1, 2), (3, 4), (5, 6)], 2: [(2, 3), (4, 5)], 3: [(3, 4)]}
+
+
+def outer_pairs(depth):
+    pairs = {}
+    for step in range(1, STEPS + 1):
+        rows = [row for row in range(step, 2 * depth + 8 - step) if not step <= row - depth < 8 - step or step == STEPS]
+        pairs[step] = [tuple(rows[i : i + 2]) for i in range(0, len(rows), 2)]
+    return pairs
+
+
 def emit_pair(member, step, pair, coef, heat, lefts, depth):
-    first_row, state, store_last = member
-    row = step + 2 * pair
+    load, store = member
     last = step == STEPS
     shift = DEEP_B - depth
-
-    def load(at):
-        if step == 1:
-            return first_row(at)
-        return state[step % 2][pl.ds(at * 32, 32), :]
-
-    rows = [load(at) for at in range(row - 1, row + 3)]
     smooth = []
-    for i in (0, 1):
-        here = rows[i + 1]
-        at = row + i + shift
-        total = (rows[i] + rows[i + 2]) + (pltpu.roll(here, 1, 1) + pltpu.roll(here, 127, 1))
+    rows = {}
+    for row in pair:
+        for at in (row - 1, row, row + 1):
+            if at not in rows:
+                rows[at] = load(step - 1, at)
+    for row in pair:
+        here = rows[row]
+        at = row + shift
+        total = (rows[row - 1] + rows[row + 1]) + (pltpu.roll(here, 1, 1) + pltpu.roll(here, 127, 1))
         keep = coef[0, pl.ds(at * 8, 8), :]
         diff = coef[1, pl.ds(at * 8, 8), :]
         smooth.append(jnp.concatenate([keep] * 4, 0) * here + jnp.concatenate([diff] * 4, 0) * total)
     high, low = split(jnp.concatenate(smooth, 1))
     right = jnp.concatenate([high, high, low], 0)
     mixed = jnp.dot(lefts[0 if step == 1 else 2 if last else 1], right, preferred_element_type=jnp.float32)
-    for i in (0, 1):
-        at = row + i
+    for i, row in enumerate(pair):
         part = mixed[:, 128 * i : 128 * (i + 1)]
-        warm = heat[1 if last else 0, pl.ds((at + shift) * 32, 32), :]
-        if last:
-            store_last(at - depth, part * (1.0 - 0.05 * (part * part)) + warm)
+        warm = heat[1 if last else 0, pl.ds((row + shift) * 32, 32), :]
+        factor = 0.05 * (part * part) if last else part * part
+        store(step, row, part * (1.0 - factor) + warm)
+
+
+def run_members(members, pairs, coef, heat, lefts, depth, lag=LAG):
+    for wave in range(len(pairs[1]) + lag * STEPS):
+        for step in pairs:
+            at = wave - lag * (step - 1)
+            if 0 <= at < len(pairs[step]):
+                for member in members:
+                    emit_pair(member, step, pairs[step][at], coef, heat, lefts, depth)
+
+
+def outer_member(depth, first_row, inner_ref, state, store_last):
+    def load(done, row):
+        if done == 0:
+            return first_row(row)
+        place = INNER.get((done, row - depth)) if inner_ref is not None else None
+        if place is not None:
+            return inner_ref[pl.ds(place * 32, 32), :]
+        return state[done % 2][pl.ds(row * 32, 32), :]
+
+    def store(step, row, value):
+        if step == STEPS:
+            store_last(row - depth, value)
         else:
-            state[(step + 1) % 2][pl.ds(at * 32, 32), :] = part * (1.0 - part * part) + warm
-
-
-def run_members(members, coef, heat, lefts, depth):
-    count = {step: depth + 4 - step for step in range(1, STEPS + 1)}
-    for wave in range(count[1] + LAG * (STEPS - 1) + 1):
-        for step in range(1, STEPS + 1):
-            pair = wave - LAG * (step - 1)
-            if 0 <= pair < count[step]:
-                for member in members:
-                    emit_pair(member, step, pair, coef, heat, lefts, depth)
+            state[step % 2][pl.ds(row * 32, 32), :] = value
+
+    return load, store
+
+
+def inner_member(own_ref, inner_ref, state):
+    def load(done, row):
+        if done == 0:
+            return strided_row(own_ref, 0, row, 8)
+        return state[done % 2][pl.ds(row * 32, 32), :]
+
+    def store(step, row, value):
+        if step < 3:
+            state[step % 2][pl.ds(row * 32, 32), :] = value
+        if (step, row) in INNER:
+            inner_ref[pl.ds(INNER[step, row] * 32, 32), :] = value
+
+    return load, store
+
+
+def all_pairs(depth):
+    return {step: [(row, row + 1) for row in range(step, 2 * depth + 8 - step, 2)] for step in range(1, STEPS + 1)}
 
 
 def prepare(pup_ref, pdown_ref, hown_ref, diff_ref, mix_ref, coef, heat, lefts):
-    for row in range(18):
+    for row in range(18) if pup_ref is not None else range(5, 13):
         if row < 5:
             value = strided_row(pup_ref, 0, row, 5)
             diff = pup_ref[pl.ds(150 + row, 1), :]
@@ -126,8 +168,21 @@
     tq_ref[j, 8:16, :] = out[8 * LEV : 8 * LEV + 8, :]
 
 
+def inner_kernel(f_ref, hown_ref, diff_ref, mix_ref, inner_ref, coef, heat, lefts, *states):
+    @pl.when(pl.program_id(0) == 0)
+    def _():
+        prepare(None, None, hown_ref, diff_ref, mix_ref, coef, heat, lefts)
+
+    def one(p, carry):
+        members = [inner_member(f_ref.at[p * 4 + q], inner_ref.at[p * 4 + q], states[2 * q : 2 * q + 2]) for q in range(4)]
+        run_members(members, INNER_PAIRS, coef, heat, lefts, 0, 2)
+        return carry
+
+    lax.fori_loop(0, 2, one, 0)
+
+
 def chunk_a_kernel(
-    f_ref, up_ref, down_ref, pup_ref, pdown_ref, hown_ref, diff_ref, mix_ref, out_ref, tq_ref, pup_out, pdown_out, coef, heat, lefts,
+    f_ref, inner_ref, up_ref, down_ref, pup_ref, pdown_ref, hown_ref, diff_ref, mix_ref, out_ref, tq_ref, pup_out, pdown_out, coef, heat, lefts,
     *states,
 ):
     @pl.when(pl.program_id(0) == 0)
@@ -142,8 +197,9 @@
             j = p * 2 + q
             base = pl.multiple_of(j * 120, 8)
             rows = first_rows(DEEP_A, up_ref, base, f_ref.at[j], down_ref, base)
-            members.append((rows, states[2 * q : 2 * q + 2], functools.partial(strided_store, out_ref.at[j])))
-        run_members(members, coef, heat, lefts, DEEP_A)
+            last = functools.partial(strided_store, out_ref.at[j])
+            members.append(outer_member(DEEP_A, rows, inner_ref.at[j], states[2 * q : 2 * q + 2], last))
+        run_members(members, outer_pairs(DEEP_A), coef, heat, lefts, DEEP_A)
         for q in range(2):
             keep_scored(tq_ref, p * 2 + q, out_ref.at[p * 2 + q])
         return carry
@@ -152,8 +208,8 @@
 
 
 def chunk_b_kernel(
-    f_ref, up_ref, down_ref, pup_ref, pdown_ref, hown_ref, diff_ref, mix_ref, prev_ref, out_ref, tq_ref, edge_ref, coef, heat, lefts,
-    *states,
+    f_ref, inner_ref, up_ref, down_ref, pup_ref, pdown_ref, hown_ref, diff_ref, mix_ref, prev_ref, out_ref, tq_ref, edge_ref,
+    coef, heat, lefts, *states,
 ):
     @pl.when(pl.program_id(0) == 0)
     def _():
@@ -176,8 +232,9 @@
             base = j * (30 * DEEP_B)
             rows = first_rows(DEEP_B, up_ref, base, f_ref.at[j], down_ref, base)
             edge_ref[j] = jnp.zeros((8, 128), jnp.float32)
-            members.append((rows, states[2 * q : 2 * q + 2], functools.partial(store_last, j)))
-        run_members(members, coef, heat, lefts, DEEP_B)
+            last = functools.partial(store_last, j)
+            members.append(outer_member(DEEP_B, rows, inner_ref.at[j], states[2 * q : 2 * q + 2], last))
+        run_members(members, outer_pairs(DEEP_B), coef, heat, lefts, DEEP_B)
         for q in range(2):
             keep_scored(tq_ref, p * 2 + q, out_ref.at[p * 2 + q])
         return carry
@@ -193,7 +250,7 @@
             up_ref[to, :] = x_ref[pl.ds(start * 8 + 8 - depth + row, 8, stride=8), :]
 
 
-def send_members(f_ref, first, count, depth, up_ref, down_ref, buf, up_buf, down_buf, sems, before):
+def send_members(f_ref, first, count, depth, up_ref, down_ref, buf, up_buf, down_buf, sems, before, after):
     rows = BLK * 30 * depth
     blocks = count // BLK
     fetches = [
@@ -222,6 +279,7 @@
 
         lax.fori_loop(0, BLK, one, 0)
         put(k * rows, rows, k)
+    after()
     for copy in copies:
         copy.wait()
 
@@ -236,8 +294,7 @@
         hot = jnp.int32(0)
         for j in range(1, 32):
             hot = jnp.where(counts_ref[base + j] >= 2, j, hot)
-        fetch = pltpu.make_async_copy(f_ref.at[hot], pieces.at[pl.ds(0, 240)], hot_sems.at[0])
-        fetch.start()
+        pltpu.make_async_copy(f_ref.at[hot], pieces.at[pl.ds(0, 240)], hot_sems.at[0]).start()
         pieces[240:256, :] = jnp.zeros((16, 128), jnp.float32)
         base = NA * 120
         send_rows(heat_ref, up_buf, down_buf, base, 5)
@@ -247,16 +304,18 @@
         up_buf[base + 155 : base + 160, :] = land[3:]
         down_buf[base + 150 : base + 155, :] = diff[:5]
         down_buf[base + 155 : base + 160, :] = land[:5]
-        fetch.wait()
+        return PARAMS
+
+    def after():
+        pltpu.make_async_copy(f_ref.at[0], pieces.at[pl.ds(0, 240)], hot_sems.at[0]).wait()
         put_pieces.start()
-        return PARAMS
-
-    send_members(f_ref, 0, NA, DEEP_A, up_ref, down_ref, buf, up_buf, down_buf, sems, before)
+
+    send_members(f_ref, 0, NA, DEEP_A, up_ref, down_ref, buf, up_buf, down_buf, sems, before, after)
     put_pieces.wait()
 
 
 def edges_b_kernel(f_ref, up_ref, down_ref, buf, up_buf, down_buf, sems):
-    send_members(f_ref, NA, NB, DEEP_B, up_ref, down_ref, buf, up_buf, down_buf, sems, lambda: 0)
+    send_members(f_ref, NA, NB, DEEP_B, up_ref, down_ref, buf, up_buf, down_buf, sems, lambda: 0, lambda: None)
 
 
 def mid_kernel(donor_ref, tq_ref, up_ref, down_ref):
@@ -315,7 +374,8 @@
 ):
     prepare(pup_ref, pdown_ref, hown_ref, diff_ref, mix_ref, coef, heat, lefts)
     rows = first_rows(DEEP_A, before_ref, 2 * NA, donor_ref, after_ref, 2 * NA)
-    run_members([(rows, (s0, s1), functools.partial(strided_store, donor))], coef, heat, lefts, DEEP_A)
+    member = outer_member(DEEP_A, rows, None, (s0, s1), functools.partial(strided_store, donor))
+    run_members([member], all_pairs(DEEP_A), coef, heat, lefts, DEEP_A)
 
     def copy(m):
         return pltpu.make_async_copy(donor, out_ref.at[m], sems.at[m])
@@ -472,15 +532,27 @@
     shared = [params, params, WHOLE, WHOLE, WHOLE]
     halo_a = pl.BlockSpec((BLK * 30 * DEEP_A, 128), lambda i: (i, 0))
     whole_params = whole((PARAMS, 128))
+    inner = call(
+        inner_kernel,
+        f32(32, 320, 128),
+        grid=(4,),
+        in_specs=[pl.BlockSpec((8, 240, 128), lambda i: (i, 0, 0))] + [WHOLE] * 3,
+        out_specs=pl.BlockSpec((8, 320, 128), lambda i: (i, 0, 0)),
+        scratch_shapes=step_scratch[:3] + [VMEM((8 * 32, 128), jnp.float32)] * 8,
+        cost_estimate=pl.CostEstimate(flops=1 << 32, bytes_accessed=10 << 20, transcendentals=0),
+        name="inner",
+    )(f, heat, diffusion, mix)
+    inner_block = pl.BlockSpec((BLK, 320, 128), lambda i: (i, 0, 0))
+    inner_b = pl.BlockSpec((BLK, 320, 128), lambda i: (i + NA // BLK, 0, 0))
     state_a, tq_a, params_up, params_down = call(
         chunk_a_kernel,
         (f32(32, 240, 128), f32(NA, 16, 128), f32(PARAMS, 128), f32(PARAMS, 128)),
         grid=(NA // BLK,),
-        in_specs=[block, halo_a, halo_a] + shared,
+        in_specs=[block, inner_block, halo_a, halo_a] + shared,
         out_specs=(block, tq_block, whole_params, whole_params),
         scratch_shapes=step_scratch,
         name="chunk_a",
-    )(f, up_a, down_a, up_a, down_a, heat, diffusion, mix)
+    )(f, inner, up_a, down_a, up_a, down_a, heat, diffusion, mix)
 
     send_up, send_down = call(
         mid_kernel, (f32(MID, 128), f32(MID, 128)), in_specs=[WHOLE, WHOLE], out_specs=(WHOLE, WHOLE), name="mid"
@@ -494,12 +566,12 @@
         chunk_b_kernel,
         (f32(32, 240, 128), f32(NB, 16, 128), f32(NB, 8, 128)),
         grid=(NB // BLK,),
-        in_specs=[block_b, halo_b, halo_b] + [WHOLE] * 5 + [hbm],
+        in_specs=[block_b, inner_b, halo_b, halo_b] + [WHOLE] * 5 + [hbm],
         out_specs=(block_b, tq_block, pl.BlockSpec((BLK, 8, 128), lambda i: (i, 0, 0))),
         scratch_shapes=step_scratch,
-        input_output_aliases={8: 0},
+        input_output_aliases={9: 0},
         name="chunk_b",
-    )(f, up_b, down_b, params_up, params_down, heat, diffusion, mix, state_a)
+    )(f, inner, up_b, down_b, params_up, params_down, heat, diffusion, mix, state_a)
 
     new_fields, sums = call(
         finish_kernel,

time: 135 us -> 131 us (0.970)
  waiting for transfers between devices: 7.69 us -> 0.02 us
  Pallas kernels: 41.5 us -> 47.2 us
  blocking collectives: 55.5 us -> 49.8 us
  starting transfers between devices: 27.9 us -> 30.7 us
    pallas_call x0 -> x1, Pallas kernels: none -> 10.1 us  [local(): call(inner_kernel, f32(32, 320, 128), grid=(4,), in_specs=[pl.BlockSpec((...]
    all_to_all x1, blocking collectives: 55.5 us -> 49.8 us  [local(): lax.all_to_all(sums.reshape(128, 1, 128), ('lat', 'grp'), 0, 0, tiled=True)]
    all_to_all x1, waiting for transfers between devices: 5.32 us -> 0.01 us  [local(): lax.all_to_all(pieces.reshape(16, 16, 128), 'grp', 0, 0, tiled=True)]
    pallas_call x1, Pallas kernels: 15.6 us -> 13.2 us  [local(): call(chunk_a_kernel, (f32(32, 240, 128), f32(NA, 16, 128), f32(PARAMS, 12...]
    ppermute x1, waiting for transfers between devices: 2.35 us -> 0.01 us  [local(): down_a = lax.ppermute(send_down_a, 'lat', down)]
    all_to_all x1, starting transfers between devices: 3.95 us -> 5.72 us  [local(): lax.all_to_all(pieces, 'grp', 0, 0, tiled=True).reshape(256, 128)]
    pallas_call x1, Pallas kernels: 11.1 us -> 9.71 us  [local(): call(chunk_b_kernel, (f32(32, 240, 128), f32(NB, 16, 128), f32(NB, 8, 128...]
  transfers between devices with their start and end apart: 8 -> 8, of which waited for: 2 -> 0; matrix products, arithmetic and copies ran while one was open for 1% -> 1% of each run, Pallas kernels for 23% -> 28%
where the time goes in v3:
time: 131 us; the launch traced here: 130 us
  blocking collectives  49.8 us (38%)
  Pallas kernels  47.2 us (36%)
  starting transfers between devices  30.7 us (23%)
    all_to_all x1, blocking collectives, local(): lax.all_to_all(sums.reshape(128, 1, 128), ('lat', 'grp'), 0, 0, tiled=True)  49.8 us
    pallas_call x1, Pallas kernels, local(): call(chunk_a_kernel, (f32(32, 240, 128), f32(NA, 16, 128), f32(PARAMS, 12...  13.2 us
    pallas_call x1, Pallas kernels, local(): call(inner_kernel, f32(32, 320, 128), grid=(4,), in_specs=[pl.BlockSpec((...  10.1 us
    pallas_call x1, Pallas kernels, local(): call(chunk_b_kernel, (f32(32, 240, 128), f32(NB, 16, 128), f32(NB, 8, 128...  9.71 us
    all_to_all x1, starting transfers between devices, local(): lax.all_to_all(pieces.reshape(16, 16, 128), 'grp', 0, 0, tiled=True)  7.78 us
    pallas_call x1, Pallas kernels, local(): call(finish_kernel, (f32(32, 240, 128), f32(128, 128)), grid=(1,), in_spe...  5.88 us
    all_to_all x1, starting transfers between devices, local(): lax.all_to_all(pieces, 'grp', 0, 0, tiled=True).reshape(256, 128)  5.72 us
    ppermute x1, starting transfers between devices, local(): up_b = lax.ppermute(send_up_b, 'lat', up)  5 us
  transfers between devices with their start and end apart: 8, of which 0 were waited for; matrix products, arithmetic and copies ran while one was open for 1% of the time, Pallas kernels for 28%

profile of v3, /device:TPU:1, one launch (start us, length us, event | category | flops | bytes accessed | tf_op | source)
XLA Modules:
  0.0 130.1 jit_solution(6295181654054125685)
XLA Ops:
  0.6 0.0 copy-start
  0.6 0.0 copy-start.7
  0.7 3.8 %shard_map.122 = (f32[256,128]{1,0:T(8,128)}, f32[2560,128]{1,0:T(8,128)}, f32[2560,128]{1,0:T(8,128)}) custom-call(s32[1]{0:T(128)} %bitcast.3.me_ref, s32[512]{0:T(512)} %counts_ref.1, f32[32,240,128]{2,1,0:T(8,128)} %bitcast.33, f32[240,128]{1,0:T(8,128)} %bitcast.21, f32[8,128]{1,0:T(8,128)} %diff_ref.9, s32[8,128]{1,0:T(8,128)} %land_ref.3), custom_call_target="tpu_custom_call" | custom-call | tf_op jit(solution)/shard_map/pallas_call | solution.py:487
  4.4 4.1 %collective-permute-start = (f32[2560,128]{1,0:T(8,128)}, f32[2560,128]{1,0:T(8,128)S(1)}, u32[]{:S(2)}, u32[]{:S(2)}) collective-permute-start(f32[2560,128]{1,0:T(8,128)} %get-tuple-element.21), channel_id=1, source_target_pairs={{0,16},{16,32},{32,48},{48,64},{64,80},{80,96},{96,112},{1,17},{17... | collective-permute-start | bytes 3932168 | tf_op jit(solution)/shard_map/ppermute | solution.py:497
  8.5 1.3 collective-permute-start.1
  9.8 2.5 %shard_map.126 = (f32[1800,128]{1,0:T(8,128)}, f32[1800,128]{1,0:T(8,128)}) custom-call(f32[32,240,128]{2,1,0:T(8,128)} %bitcast.34), custom_call_target="tpu_custom_call" | custom-call | tf_op jit(solution)/shard_map/pallas_call | solution.py:504
  12.4 5.0 %collective-permute-start.4 = (f32[1800,128]{1,0:T(8,128)}, f32[1800,128]{1,0:T(8,128)}, u32[]{:S(2)}, u32[]{:S(2)}) collective-permute-start(f32[1800,128]{1,0:T(8,128)} %get-tuple-element.27), channel_id=1, source_target_pairs={{0,16},{16,32},{32,48},{48,64},{64,80},{80,96},{96,112},{1,17},{17... | collective-permute-start | bytes 2764808 | tf_op jit(solution)/shard_map/ppermute | solution.py:512
  17.4 1.3 collective-permute-start.5
  18.7 7.8 %all-to-all-start = ((f32[16,16,128]{2,1,0:T(8,128)}), f32[16,16,128]{2,1,0:T(8,128)S(1)}, u32[]{:S(2)}, u32[]{:S(2)}) async-start(f32[16,16,128]{2,1,0:T(8,128)} %bitcast.4), calls=%async_computation | async-start | bytes 262144 | tf_op jit(solution)/shard_map/all_to_all | solution.py:496
  26.4 0.0 copy-done.7
  26.5 0.1 pad.1.clone
  26.6 0.7 fusion.mix_ref
  27.2 0.0 copy-start.8
  27.2 0.0 copy-start.9
  27.2 0.0 copy-start.6
  27.2 0.0 copy-start.1
  27.2 0.0 copy-start.2
  27.3 0.0 copy-start.4
  27.3 10.1 %shard_map.121.inner_ref = f32[32,320,128]{2,1,0:T(8,128)} custom-call(f32[32,240,128]{2,1,0:T(8,128)} %bitcast.35, f32[240,128]{1,0:T(8,128)} %bitcast.22, f32[8,128]{1,0:T(8,128)} %diff_ref.9, f32[32,32]{1,0:T(8,128)} %fusion.mix_ref), custom_call_target="tpu_custom_call" | custom-call | flops 4294967296 | bytes 10485760 | tf_op jit(solution)/shard_map/pallas_call | solution.py:535
  37.3 0.0 copy-done.8
  37.3 0.1 reshape.65.counts_ref
  37.4 0.0 copy-done.9
  37.4 0.1 reshape.69.source_ref
  37.5 0.1 fusion.3.index_ref
  37.6 0.0 all-to-all-done.pieces_ref
  37.6 1.2 shard_map.124
  38.8 5.7 %all-to-all-start.1 = ((f32[16,16,128]{2,1,0:T(8,128)}), f32[16,16,128]{2,1,0:T(8,128)S(1)}, u32[]{:S(2)}, u32[]{:S(2)}) async-start(f32[16,16,128]{2,1,0:T(8,128)} %shard_map.124), calls=%async_computation.1 | async-start | bytes 262144 | tf_op jit(solution)/shard_map/all_to_all | solution.py:502
  44.6 0.0 copy-done
  44.6 0.0 copy-done.6
  44.6 0.2 convolution_bitcast_fusion
  44.8 0.1 reshape.77.weight_ref
  44.9 0.0 collective-permute-done.up_ref.pup_ref
  44.9 0.0 collective-permute-done.1.down_ref.pdown_ref
  44.9 0.0 copy-done.1
  45.0 0.0 copy-done.2
  45.0 0.0 copy-done.4
  45.0 13.2 %shard_map.123 = (f32[32,240,128]{2,1,0:T(8,128)}, f32[20,16,128]{2,1,0:T(8,128)S(1)}, f32[160,128]{1,0:T(8,128)S(1)}, f32[160,128]{1,0:T(8,128)S(1)}) custom-call(f32[32,240,128]{2,1,0:T(8,128)} %bitcast.36, f32[32,320,128]{2,1,0:T(8,128)} %shard_map.121.inner_ref, f32[2560,128]{1,0:T(8,128)S(1)} %collective-permute-done.up_ref.pup_ref, ...), custom_call_target="tpu_custom_call" | custom-call | tf_op jit(solution)/shard_map/pallas_call | solution.py:547
  58.2 0.0 all-to-all-done.1
  58.2 4.3 %collective-permute-start.2 = (f32[160,128]{1,0:T(8,128)S(1)}, f32[160,128]{1,0:T(8,128)S(1)}, u32[]{:S(2)}, u32[]{:S(2)}) collective-permute-start(f32[160,128]{1,0:T(8,128)S(1)} %get-tuple-element.25), channel_id=1, source_target_pairs={{0,16},{16,32},{32,48},{48,64},{64,80},{80,96},{96,112},{1,17},{17... | collective-permute-start | bytes 245768 | tf_op jit(solution)/shard_map/ppermute | solution.py:560
  62.5 1.3 collective-permute-start.3
  63.8 0.0 collective-permute-done.4.up_ref
  63.8 0.0 collective-permute-done.5.down_ref
  63.8 0.0 copy-start.3
  63.9 0.0 copy-start.5
  63.9 9.7 %shard_map.127 = (f32[32,240,128]{2,1,0:T(8,128)}, f32[12,16,128]{2,1,0:T(8,128)S(1)}, f32[12,8,128]{2,1,0:T(8,128)S(1)}) custom-call(f32[32,240,128]{2,1,0:T(8,128)} %bitcast.37, f32[32,320,128]{2,1,0:T(8,128)} %shard_map.121.inner_ref, f32[1800,128]{1,0:T(8,128)} %collective-permute-done.4.up_ref, ...), custom_call_target="tpu_custom_call", output_to_operand_aliasing={{0}: (9, {})} | custom-call | tf_op jit(solution)/shard_map/pallas_call | solution.py:565
  73.6 0.0 collective-permute-done.2.before_ref
  73.6 0.0 collective-permute-done.3.after_ref
  73.6 0.0 copy-done.3
  73.6 0.0 copy-done.5
  73.6 5.9 %shard_map.128 = (f32[32,240,128]{2,1,0:T(8,128)}, f32[128,128]{1,0:T(8,128)S(1)}) custom-call(s32[32]{0:T(128)S(1)} %fusion.5.killed_ref, f32[20,16,128]{2,1,0:T(8,128)S(1)} %get-tuple-element.23.tqa_ref, f32[160,128]{1,0:T(8,128)S(1)} %collective-permute-done.2.before_ref, ...), custom_call_target="tpu_custom_call", output_to_operand_aliasing={{0}: (15, {})} | custom-call | tf_op jit(solution)/shard_map/pallas_call | solution.py:576
  79.5 49.8 %all_to_all.15 = f32[128,1,128]{2,1,0:T(1,128)S(1)} all-to-all(f32[128,1,128]{2,1,0:T(1,128)S(1)} %bitcast.31), channel_id=1, replica_groups=mesh['lat'=8,'grp'=16] {'lat','grp'}, dimensions={0} | all-to-all | bytes 131072 | tf_op jit(solution)/shard_map/all_to_all | solution.py:597
  129.3 0.8 shard_map.129
  (6 shorter events, 0.1 us)
Async XLA Ops:
  0.6 43.9 %copy-start = (f32[32,27]{1,0:T(8,128)S(1)}, f32[32,27]{1,0:T(8,128)}, u32[]{:S(2)}) copy-start(f32[32,27]{1,0:T(8,128)} %param.15) | copy-start | bytes 10372
  0.6 25.8 %copy-start.7 = (f32[30,30]{1,0:T(8,128)S(1)}, f32[30,30]{1,0:T(8,128)}, u32[]{:S(2)}) copy-start(f32[30,30]{1,0:T(8,128)} %param.12) | copy-start | bytes 10804
  4.4 40.5 %collective-permute-start = (f32[2560,128]{1,0:T(8,128)}, f32[2560,128]{1,0:T(8,128)S(1)}, u32[]{:S(2)}, u32[]{:S(2)}) collective-permute-start(f32[2560,128]{1,0:T(8,128)} %get-tuple-element.21), channel_id=1, source_target_pairs={{0,16},{16,32},{32,48},{48,64},{64,80},{80,96},{96,112},{1,17},{17... | collective-permute-start | bytes 3932168 | tf_op jit(solution)/shard_map/ppermute | solution.py:497
  8.5 36.4 %collective-permute-start.1 = (f32[2560,128]{1,0:T(8,128)}, f32[2560,128]{1,0:T(8,128)S(1)}, u32[]{:S(2)}, u32[]{:S(2)}) collective-permute-start(f32[2560,128]{1,0:T(8,128)} %get-tuple-element.22), channel_id=1, source_target_pairs={{16,0},{32,16},{48,32},{64,48},{80,64},{96,80},{112,96},{17,1},{33... | collective-permute-start | bytes 3932168 | tf_op jit(solution)/shard_map/ppermute | solution.py:498
  12.4 51.5 %collective-permute-start.4 = (f32[1800,128]{1,0:T(8,128)}, f32[1800,128]{1,0:T(8,128)}, u32[]{:S(2)}, u32[]{:S(2)}) collective-permute-start(f32[1800,128]{1,0:T(8,128)} %get-tuple-element.27), channel_id=1, source_target_pairs={{0,16},{16,32},{32,48},{48,64},{64,80},{80,96},{96,112},{1,17},{17... | collective-permute-start | bytes 2764808 | tf_op jit(solution)/shard_map/ppermute | solution.py:512
  17.4 46.5 %collective-permute-start.5 = (f32[1800,128]{1,0:T(8,128)}, f32[1800,128]{1,0:T(8,128)}, u32[]{:S(2)}, u32[]{:S(2)}) collective-permute-start(f32[1800,128]{1,0:T(8,128)} %get-tuple-element.28), channel_id=1, source_target_pairs={{16,0},{32,16},{48,32},{64,48},{80,64},{96,80},{112,96},{17,1},{33... | collective-permute-start | bytes 2764808 | tf_op jit(solution)/shard_map/ppermute | solution.py:513
  18.7 19.0 %all-to-all-start = ((f32[16,16,128]{2,1,0:T(8,128)}), f32[16,16,128]{2,1,0:T(8,128)S(1)}, u32[]{:S(2)}, u32[]{:S(2)}) async-start(f32[16,16,128]{2,1,0:T(8,128)} %bitcast.4), calls=%async_computation | async-start | bytes 262144 | tf_op jit(solution)/shard_map/all_to_all | solution.py:496
  27.2 10.1 %copy-start.8 = (s32[512]{0:T(512)S(1)}, s32[512]{0:T(512)}, u32[]{:S(2)}) copy-start(s32[512]{0:T(512)} %counts_ref.1) | copy-start | bytes 6148
  27.2 10.2 %copy-start.9 = (s32[512]{0:T(512)S(1)}, s32[512]{0:T(512)}, u32[]{:S(2)}) copy-start(s32[512]{0:T(512)} %param.18) | copy-start | bytes 6148
  27.2 17.3 %copy-start.6 = (f32[27,768]{1,0:T(8,128)S(1)}, f32[27,768]{1,0:T(8,128)}, u32[]{:S(2)}) copy-start(f32[27,768]{1,0:T(8,128)} %constant.35.clone) | copy-start | bytes 248836
  27.2 17.7 %copy-start.1 = (f32[30,8,128]{2,1,0:T(8,128)S(1)}, f32[30,8,128]{2,1,0:T(8,128)}, u32[]{:S(2)}) copy-start(f32[30,8,128]{2,1,0:T(8,128)} %param.13) | copy-start | bytes 368644
  27.2 17.7 %copy-start.2 = (f32[32,32]{1,0:T(8,128)S(1)}, f32[32,32]{1,0:T(8,128)}, u32[]{:S(2)}) copy-start(f32[32,32]{1,0:T(8,128)} %fusion.mix_ref) | copy-start | bytes 12292
  27.3 17.7 %copy-start.4 = (f32[8,128]{1,0:T(8,128)S(1)}, f32[8,128]{1,0:T(8,128)}, u32[]{:S(2)}) copy-start(f32[8,128]{1,0:T(8,128)} %diff_ref.9) | copy-start | bytes 12292
  38.8 19.3 %all-to-all-start.1 = ((f32[16,16,128]{2,1,0:T(8,128)}), f32[16,16,128]{2,1,0:T(8,128)S(1)}, u32[]{:S(2)}, u32[]{:S(2)}) async-start(f32[16,16,128]{2,1,0:T(8,128)} %shard_map.124), calls=%async_computation.1 | async-start | bytes 262144 | tf_op jit(solution)/shard_map/all_to_all | solution.py:502
  58.2 15.4 %collective-permute-start.2 = (f32[160,128]{1,0:T(8,128)S(1)}, f32[160,128]{1,0:T(8,128)S(1)}, u32[]{:S(2)}, u32[]{:S(2)}) collective-permute-start(f32[160,128]{1,0:T(8,128)S(1)} %get-tuple-element.25), channel_id=1, source_target_pairs={{0,16},{16,32},{32,48},{48,64},{64,80},{80,96},{96,112},{1,17},{17... | collective-permute-start | bytes 245768 | tf_op jit(solution)/shard_map/ppermute | solution.py:560
  62.5 11.1 %collective-permute-start.3 = (f32[160,128]{1,0:T(8,128)S(1)}, f32[160,128]{1,0:T(8,128)S(1)}, u32[]{:S(2)}, u32[]{:S(2)}) collective-permute-start(f32[160,128]{1,0:T(8,128)S(1)} %get-tuple-element.26), channel_id=1, source_target_pairs={{16,0},{32,16},{48,32},{64,48},{80,64},{96,80},{112,96},{17,1},{33... | collective-permute-start | bytes 245768 | tf_op jit(solution)/shard_map/ppermute | solution.py:561
  63.8 9.7 %copy-start.3 = (f32[32,8,128]{2,1,0:T(8,128)S(1)}, f32[32,8,128]{2,1,0:T(8,128)}, u32[]{:S(2)}) copy-start(f32[32,8,128]{2,1,0:T(8,128)} %param.16) | copy-start | bytes 393220
  63.9 9.7 %copy-start.5 = (s32[8,128]{1,0:T(8,128)S(1)}, s32[8,128]{1,0:T(8,128)}, u32[]{:S(2)}) copy-start(s32[8,128]{1,0:T(8,128)} %land_ref.3) | copy-start | bytes 12292

commit v4 on v3

--- a/solution.py
+++ b/solution.py
@@ -193,18 +193,18 @@
 
     def one(p, carry):
         members = []
-        for q in range(2):
-            j = p * 2 + q
+        for q in range(4):
+            j = p * 4 + q
             base = pl.multiple_of(j * 120, 8)
             rows = first_rows(DEEP_A, up_ref, base, f_ref.at[j], down_ref, base)
             last = functools.partial(strided_store, out_ref.at[j])
             members.append(outer_member(DEEP_A, rows, inner_ref.at[j], states[2 * q : 2 * q + 2], last))
         run_members(members, outer_pairs(DEEP_A), coef, heat, lefts, DEEP_A)
-        for q in range(2):
-            keep_scored(tq_ref, p * 2 + q, out_ref.at[p * 2 + q])
+        for q in range(4):
+            keep_scored(tq_ref, p * 4 + q, out_ref.at[p * 4 + q])
         return carry
 
-    lax.fori_loop(0, BLK // 2, one, 0)
+    lax.fori_loop(0, BLK // 4, one, 0)
 
 
 def chunk_b_kernel(
@@ -227,19 +227,19 @@
 
     def one(p, carry):
         members = []
-        for q in range(2):
-            j = p * 2 + q
+        for q in range(4):
+            j = p * 4 + q
             base = j * (30 * DEEP_B)
             rows = first_rows(DEEP_B, up_ref, base, f_ref.at[j], down_ref, base)
             edge_ref[j] = jnp.zeros((8, 128), jnp.float32)
             last = functools.partial(store_last, j)
             members.append(outer_member(DEEP_B, rows, inner_ref.at[j], states[2 * q : 2 * q + 2], last))
         run_members(members, outer_pairs(DEEP_B), coef, heat, lefts, DEEP_B)
-        for q in range(2):
-            keep_scored(tq_ref, p * 2 + q, out_ref.at[p * 2 + q])
+        for q in range(4):
+            keep_scored(tq_ref, p * 4 + q, out_ref.at[p * 4 + q])
         return carry
 
-    lax.fori_loop(0, BLK // 2, one, 0)
+    lax.fori_loop(0, BLK // 4, one, 0)
 
 
 def send_rows(x_ref, up_ref, down_ref, base, depth):
@@ -528,7 +528,7 @@
         VMEM((2, 18 * 8, 128), jnp.float32),
         VMEM((2, 18 * 32, 128), jnp.float32),
         VMEM((3, 32, 96), jnp.bfloat16),
-    ] + [VMEM((18 * 32, 128), jnp.float32)] * 4
+    ] + [VMEM((18 * 32, 128), jnp.float32)] * 8
     shared = [params, params, WHOLE, WHOLE, WHOLE]
     halo_a = pl.BlockSpec((BLK * 30 * DEEP_A, 128), lambda i: (i, 0))
     whole_params = whole((PARAMS, 128))
@@ -579,7 +579,7 @@
         grid=(1,),
         in_specs=[SCALAR] + [WHOLE] * 14 + [hbm],
         out_specs=(hbm, WHOLE),
-        scratch_shapes=step_scratch[:-2]
+        scratch_shapes=step_scratch[:5]
         + [
             VMEM((240, 128), jnp.float32),
             VMEM(((NA + 7) // 8 * 64, 128), jnp.float32),

time: 131 us -> 125 us (0.954)
  Pallas kernels: 47.2 us -> 41.2 us
    pallas_call x1, Pallas kernels: 13.2 us -> 9.48 us  [local(): call(chunk_a_kernel, (f32(32, 240, 128), f32(NA, 16, 128), f32(PARAMS, 12...]
    pallas_call x1, Pallas kernels: 9.71 us -> 7.36 us  [local(): call(chunk_b_kernel, (f32(32, 240, 128), f32(NB, 16, 128), f32(NB, 8, 128...]
  transfers between devices with their start and end apart: 8 -> 8, of which waited for: 0 -> 0; matrix products, arithmetic and copies ran while one was open for 1% -> 1% of each run, Pallas kernels for 28% -> 25%
where the time goes in v4:
time: 125 us; the launch traced here: 124 us
  blocking collectives  49.8 us (40%)
  Pallas kernels  41.2 us (33%)
  starting transfers between devices  30.7 us (25%)
    all_to_all x1, blocking collectives, local(): lax.all_to_all(sums.reshape(128, 1, 128), ('lat', 'grp'), 0, 0, tiled=True)  49.8 us
    pallas_call x1, Pallas kernels, local(): call(inner_kernel, f32(32, 320, 128), grid=(4,), in_specs=[pl.BlockSpec((...  10.1 us
    pallas_call x1, Pallas kernels, local(): call(chunk_a_kernel, (f32(32, 240, 128), f32(NA, 16, 128), f32(PARAMS, 12...  9.48 us
    all_to_all x1, starting transfers between devices, local(): lax.all_to_all(pieces.reshape(16, 16, 128), 'grp', 0, 0, tiled=True)  7.78 us
    pallas_call x1, Pallas kernels, local(): call(chunk_b_kernel, (f32(32, 240, 128), f32(NB, 16, 128), f32(NB, 8, 128...  7.36 us
    pallas_call x1, Pallas kernels, local(): call(finish_kernel, (f32(32, 240, 128), f32(128, 128)), grid=(1,), in_spe...  5.88 us
    all_to_all x1, starting transfers between devices, local(): lax.all_to_all(pieces, 'grp', 0, 0, tiled=True).reshape(256, 128)  5.72 us
    ppermute x1, starting transfers between devices, local(): up_b = lax.ppermute(send_up_b, 'lat', up)  5 us
  transfers between devices with their start and end apart: 8, of which 0 were waited for; matrix products, arithmetic and copies ran while one was open for 1% of the time, Pallas kernels for 25%

profile of v4, /device:TPU:1, one launch (start us, length us, event | category | flops | bytes accessed | tf_op | source)
XLA Modules:
  0.0 124.0 jit_solution(12568179915550183645)
XLA Ops:
  0.6 0.0 copy-start
  0.6 0.0 copy-start.7
  0.7 3.8 %shard_map.122 = (f32[256,128]{1,0:T(8,128)}, f32[2560,128]{1,0:T(8,128)}, f32[2560,128]{1,0:T(8,128)}) custom-call(s32[1]{0:T(128)} %bitcast.3.me_ref, s32[512]{0:T(512)} %counts_ref.1, f32[32,240,128]{2,1,0:T(8,128)} %bitcast.33, f32[240,128]{1,0:T(8,128)} %bitcast.21, f32[8,128]{1,0:T(8,128)} %diff_ref.9, s32[8,128]{1,0:T(8,128)} %land_ref.3), custom_call_target="tpu_custom_call" | custom-call | tf_op jit(solution)/shard_map/pallas_call | solution.py:487
  4.4 4.1 %collective-permute-start = (f32[2560,128]{1,0:T(8,128)}, f32[2560,128]{1,0:T(8,128)S(1)}, u32[]{:S(2)}, u32[]{:S(2)}) collective-permute-start(f32[2560,128]{1,0:T(8,128)} %get-tuple-element.21), channel_id=1, source_target_pairs={{0,16},{16,32},{32,48},{48,64},{64,80},{80,96},{96,112},{1,17},{17... | collective-permute-start | bytes 3932168 | tf_op jit(solution)/shard_map/ppermute | solution.py:497
  8.5 1.3 %collective-permute-start.1 = (f32[2560,128]{1,0:T(8,128)}, f32[2560,128]{1,0:T(8,128)S(1)}, u32[]{:S(2)}, u32[]{:S(2)}) collective-permute-start(f32[2560,128]{1,0:T(8,128)} %get-tuple-element.22), channel_id=1, source_target_pairs={{16,0},{32,16},{48,32},{64,48},{80,64},{96,80},{112,96},{17,1},{33... | collective-permute-start | bytes 3932168 | tf_op jit(solution)/shard_map/ppermute | solution.py:498
  9.8 2.5 %shard_map.126 = (f32[1800,128]{1,0:T(8,128)}, f32[1800,128]{1,0:T(8,128)}) custom-call(f32[32,240,128]{2,1,0:T(8,128)} %bitcast.34), custom_call_target="tpu_custom_call" | custom-call | tf_op jit(solution)/shard_map/pallas_call | solution.py:504
  12.4 5.0 %collective-permute-start.4 = (f32[1800,128]{1,0:T(8,128)}, f32[1800,128]{1,0:T(8,128)}, u32[]{:S(2)}, u32[]{:S(2)}) collective-permute-start(f32[1800,128]{1,0:T(8,128)} %get-tuple-element.27), channel_id=1, source_target_pairs={{0,16},{16,32},{32,48},{48,64},{64,80},{80,96},{96,112},{1,17},{17... | collective-permute-start | bytes 2764808 | tf_op jit(solution)/shard_map/ppermute | solution.py:512
  17.4 1.3 %collective-permute-start.5 = (f32[1800,128]{1,0:T(8,128)}, f32[1800,128]{1,0:T(8,128)}, u32[]{:S(2)}, u32[]{:S(2)}) collective-permute-start(f32[1800,128]{1,0:T(8,128)} %get-tuple-element.28), channel_id=1, source_target_pairs={{16,0},{32,16},{48,32},{64,48},{80,64},{96,80},{112,96},{17,1},{33... | collective-permute-start | bytes 2764808 | tf_op jit(solution)/shard_map/ppermute | solution.py:513
  18.7 7.8 %all-to-all-start = ((f32[16,16,128]{2,1,0:T(8,128)}), f32[16,16,128]{2,1,0:T(8,128)S(1)}, u32[]{:S(2)}, u32[]{:S(2)}) async-start(f32[16,16,128]{2,1,0:T(8,128)} %bitcast.4), calls=%async_computation | async-start | bytes 262144 | tf_op jit(solution)/shard_map/all_to_all | solution.py:496
  26.4 0.0 copy-done.7
  26.5 0.1 pad.1.clone
  26.6 0.7 fusion.mix_ref
  27.2 0.0 copy-start.8
  27.2 0.0 copy-start.9
  27.2 0.0 copy-start.6
  27.2 0.0 copy-start.1
  27.2 0.0 copy-start.2
  27.3 0.0 copy-start.4
  27.3 10.1 %shard_map.121.inner_ref = f32[32,320,128]{2,1,0:T(8,128)} custom-call(f32[32,240,128]{2,1,0:T(8,128)} %bitcast.35, f32[240,128]{1,0:T(8,128)} %bitcast.22, f32[8,128]{1,0:T(8,128)} %diff_ref.9, f32[32,32]{1,0:T(8,128)} %fusion.mix_ref), custom_call_target="tpu_custom_call" | custom-call | flops 4294967296 | bytes 10485760 | tf_op jit(solution)/shard_map/pallas_call | solution.py:535
  37.3 0.0 copy-done.8
  37.3 0.1 reshape.65.counts_ref
  37.4 0.0 copy-done.9
  37.4 0.1 reshape.69.source_ref
  37.5 0.1 fusion.3.index_ref
  37.6 0.0 all-to-all-done.pieces_ref
  37.6 1.2 shard_map.124
  38.8 5.7 %all-to-all-start.1 = ((f32[16,16,128]{2,1,0:T(8,128)}), f32[16,16,128]{2,1,0:T(8,128)S(1)}, u32[]{:S(2)}, u32[]{:S(2)}) async-start(f32[16,16,128]{2,1,0:T(8,128)} %shard_map.124), calls=%async_computation.1 | async-start | bytes 262144 | tf_op jit(solution)/shard_map/all_to_all | solution.py:502
  44.6 0.0 copy-done
  44.6 0.0 copy-done.6
  44.6 0.2 convolution_bitcast_fusion
  44.8 0.1 reshape.77.weight_ref
  44.9 0.0 collective-permute-done.up_ref.pup_ref
  44.9 0.0 collective-permute-done.1.down_ref.pdown_ref
  44.9 0.0 copy-done.1
  45.0 0.0 copy-done.2
  45.0 0.0 copy-done.4
  45.0 9.5 %shard_map.123 = (f32[32,240,128]{2,1,0:T(8,128)}, f32[20,16,128]{2,1,0:T(8,128)S(1)}, f32[160,128]{1,0:T(8,128)S(1)}, f32[160,128]{1,0:T(8,128)S(1)}) custom-call(f32[32,240,128]{2,1,0:T(8,128)} %bitcast.36, f32[32,320,128]{2,1,0:T(8,128)} %shard_map.121.inner_ref, f32[2560,128]{1,0:T(8,128)S(1)} %collective-permute-done.up_ref.pup_ref, ...), custom_call_target="tpu_custom_call" | custom-call | tf_op jit(solution)/shard_map/pallas_call | solution.py:547
  54.4 0.0 all-to-all-done.1
  54.5 4.3 %collective-permute-start.2 = (f32[160,128]{1,0:T(8,128)S(1)}, f32[160,128]{1,0:T(8,128)S(1)}, u32[]{:S(2)}, u32[]{:S(2)}) collective-permute-start(f32[160,128]{1,0:T(8,128)S(1)} %get-tuple-element.25), channel_id=1, source_target_pairs={{0,16},{16,32},{32,48},{48,64},{64,80},{80,96},{96,112},{1,17},{17... | collective-permute-start | bytes 245768 | tf_op jit(solution)/shard_map/ppermute | solution.py:560
  58.8 1.3 %collective-permute-start.3 = (f32[160,128]{1,0:T(8,128)S(1)}, f32[160,128]{1,0:T(8,128)S(1)}, u32[]{:S(2)}, u32[]{:S(2)}) collective-permute-start(f32[160,128]{1,0:T(8,128)S(1)} %get-tuple-element.26), channel_id=1, source_target_pairs={{16,0},{32,16},{48,32},{64,48},{80,64},{96,80},{112,96},{17,1},{33... | collective-permute-start | bytes 245768 | tf_op jit(solution)/shard_map/ppermute | solution.py:561
  60.1 0.0 collective-permute-done.4.up_ref
  60.1 0.0 collective-permute-done.5.down_ref
  60.1 0.0 copy-start.3
  60.1 0.0 copy-start.5
  60.1 7.4 %shard_map.127 = (f32[32,240,128]{2,1,0:T(8,128)}, f32[12,16,128]{2,1,0:T(8,128)S(1)}, f32[12,8,128]{2,1,0:T(8,128)S(1)}) custom-call(f32[32,240,128]{2,1,0:T(8,128)} %bitcast.37, f32[32,320,128]{2,1,0:T(8,128)} %shard_map.121.inner_ref, f32[1800,128]{1,0:T(8,128)} %collective-permute-done.4.up_ref, ...), custom_call_target="tpu_custom_call", output_to_operand_aliasing={{0}: (9, {})} | custom-call | tf_op jit(solution)/shard_map/pallas_call | solution.py:565
  67.5 0.0 collective-permute-done.2.before_ref
  67.5 0.0 collective-permute-done.3.after_ref
  67.5 0.0 copy-done.3
  67.5 0.0 copy-done.5
  67.5 5.9 %shard_map.128 = (f32[32,240,128]{2,1,0:T(8,128)}, f32[128,128]{1,0:T(8,128)S(1)}) custom-call(s32[32]{0:T(128)S(1)} %fusion.5.killed_ref, f32[20,16,128]{2,1,0:T(8,128)S(1)} %get-tuple-element.23.tqa_ref, f32[160,128]{1,0:T(8,128)S(1)} %collective-permute-done.2.before_ref, ...), custom_call_target="tpu_custom_call", output_to_operand_aliasing={{0}: (15, {})} | custom-call | tf_op jit(solution)/shard_map/pallas_call | solution.py:576
  73.4 49.8 %all_to_all.15 = f32[128,1,128]{2,1,0:T(1,128)S(1)} all-to-all(f32[128,1,128]{2,1,0:T(1,128)S(1)} %bitcast.31), channel_id=1, replica_groups=mesh['lat'=8,'grp'=16] {'lat','grp'}, dimensions={0} | all-to-all | bytes 131072 | tf_op jit(solution)/shard_map/all_to_all | solution.py:597
  123.2 0.8 shard_map.129
  (6 shorter events, 0.1 us)
Async XLA Ops:
  0.6 43.9 %copy-start = (f32[32,27]{1,0:T(8,128)S(1)}, f32[32,27]{1,0:T(8,128)}, u32[]{:S(2)}) copy-start(f32[32,27]{1,0:T(8,128)} %param.15) | copy-start | bytes 10372
  0.6 25.8 %copy-start.7 = (f32[30,30]{1,0:T(8,128)S(1)}, f32[30,30]{1,0:T(8,128)}, u32[]{:S(2)}) copy-start(f32[30,30]{1,0:T(8,128)} %param.12) | copy-start | bytes 10804
  4.4 40.5 %collective-permute-start = (f32[2560,128]{1,0:T(8,128)}, f32[2560,128]{1,0:T(8,128)S(1)}, u32[]{:S(2)}, u32[]{:S(2)}) collective-permute-start(f32[2560,128]{1,0:T(8,128)} %get-tuple-element.21), channel_id=1, source_target_pairs={{0,16},{16,32},{32,48},{48,64},{64,80},{80,96},{96,112},{1,17},{17... | collective-permute-start | bytes 3932168 | tf_op jit(solution)/shard_map/ppermute | solution.py:497
  8.5 36.4 %collective-permute-start.1 = (f32[2560,128]{1,0:T(8,128)}, f32[2560,128]{1,0:T(8,128)S(1)}, u32[]{:S(2)}, u32[]{:S(2)}) collective-permute-start(f32[2560,128]{1,0:T(8,128)} %get-tuple-element.22), channel_id=1, source_target_pairs={{16,0},{32,16},{48,32},{64,48},{80,64},{96,80},{112,96},{17,1},{33... | collective-permute-start | bytes 3932168 | tf_op jit(solution)/shard_map/ppermute | solution.py:498
  12.4 47.7 %collective-permute-start.4 = (f32[1800,128]{1,0:T(8,128)}, f32[1800,128]{1,0:T(8,128)}, u32[]{:S(2)}, u32[]{:S(2)}) collective-permute-start(f32[1800,128]{1,0:T(8,128)} %get-tuple-element.27), channel_id=1, source_target_pairs={{0,16},{16,32},{32,48},{48,64},{64,80},{80,96},{96,112},{1,17},{17... | collective-permute-start | bytes 2764808 | tf_op jit(solution)/shard_map/ppermute | solution.py:512
  17.4 42.7 %collective-permute-start.5 = (f32[1800,128]{1,0:T(8,128)}, f32[1800,128]{1,0:T(8,128)}, u32[]{:S(2)}, u32[]{:S(2)}) collective-permute-start(f32[1800,128]{1,0:T(8,128)} %get-tuple-element.28), channel_id=1, source_target_pairs={{16,0},{32,16},{48,32},{64,48},{80,64},{96,80},{112,96},{17,1},{33... | collective-permute-start | bytes 2764808 | tf_op jit(solution)/shard_map/ppermute | solution.py:513
  18.7 19.0 %all-to-all-start = ((f32[16,16,128]{2,1,0:T(8,128)}), f32[16,16,128]{2,1,0:T(8,128)S(1)}, u32[]{:S(2)}, u32[]{:S(2)}) async-start(f32[16,16,128]{2,1,0:T(8,128)} %bitcast.4), calls=%async_computation | async-start | bytes 262144 | tf_op jit(solution)/shard_map/all_to_all | solution.py:496
  27.2 10.1 %copy-start.8 = (s32[512]{0:T(512)S(1)}, s32[512]{0:T(512)}, u32[]{:S(2)}) copy-start(s32[512]{0:T(512)} %counts_ref.1) | copy-start | bytes 6148
  27.2 10.2 %copy-start.9 = (s32[512]{0:T(512)S(1)}, s32[512]{0:T(512)}, u32[]{:S(2)}) copy-start(s32[512]{0:T(512)} %param.18) | copy-start | bytes 6148
  27.2 17.3 %copy-start.6 = (f32[27,768]{1,0:T(8,128)S(1)}, f32[27,768]{1,0:T(8,128)}, u32[]{:S(2)}) copy-start(f32[27,768]{1,0:T(8,128)} %constant.35.clone) | copy-start | bytes 248836
  27.2 17.7 %copy-start.1 = (f32[30,8,128]{2,1,0:T(8,128)S(1)}, f32[30,8,128]{2,1,0:T(8,128)}, u32[]{:S(2)}) copy-start(f32[30,8,128]{2,1,0:T(8,128)} %param.13) | copy-start | bytes 368644
  27.2 17.7 %copy-start.2 = (f32[32,32]{1,0:T(8,128)S(1)}, f32[32,32]{1,0:T(8,128)}, u32[]{:S(2)}) copy-start(f32[32,32]{1,0:T(8,128)} %fusion.mix_ref) | copy-start | bytes 12292
  27.3 17.7 %copy-start.4 = (f32[8,128]{1,0:T(8,128)S(1)}, f32[8,128]{1,0:T(8,128)}, u32[]{:S(2)}) copy-start(f32[8,128]{1,0:T(8,128)} %diff_ref.9) | copy-start | bytes 12292
  38.8 15.6 %all-to-all-start.1 = ((f32[16,16,128]{2,1,0:T(8,128)}), f32[16,16,128]{2,1,0:T(8,128)S(1)}, u32[]{:S(2)}, u32[]{:S(2)}) async-start(f32[16,16,128]{2,1,0:T(8,128)} %shard_map.124), calls=%async_computation.1 | async-start | bytes 262144 | tf_op jit(solution)/shard_map/all_to_all | solution.py:502
  54.5 13.0 %collective-permute-start.2 = (f32[160,128]{1,0:T(8,128)S(1)}, f32[160,128]{1,0:T(8,128)S(1)}, u32[]{:S(2)}, u32[]{:S(2)}) collective-permute-start(f32[160,128]{1,0:T(8,128)S(1)} %get-tuple-element.25), channel_id=1, source_target_pairs={{0,16},{16,32},{32,48},{48,64},{64,80},{80,96},{96,112},{1,17},{17... | collective-permute-start | bytes 245768 | tf_op jit(solution)/shard_map/ppermute | solution.py:560
  58.8 8.7 %collective-permute-start.3 = (f32[160,128]{1,0:T(8,128)S(1)}, f32[160,128]{1,0:T(8,128)S(1)}, u32[]{:S(2)}, u32[]{:S(2)}) collective-permute-start(f32[160,128]{1,0:T(8,128)S(1)} %get-tuple-element.26), channel_id=1, source_target_pairs={{16,0},{32,16},{48,32},{64,48},{80,64},{96,80},{112,96},{17,1},{33... | collective-permute-start | bytes 245768 | tf_op jit(solution)/shard_map/ppermute | solution.py:561
  60.1 7.4 %copy-start.3 = (f32[32,8,128]{2,1,0:T(8,128)S(1)}, f32[32,8,128]{2,1,0:T(8,128)}, u32[]{:S(2)}) copy-start(f32[32,8,128]{2,1,0:T(8,128)} %param.16) | copy-start | bytes 393220
  60.1 7.4 %copy-start.5 = (s32[8,128]{1,0:T(8,128)S(1)}, s32[8,128]{1,0:T(8,128)}, u32[]{:S(2)}) copy-start(s32[8,128]{1,0:T(8,128)} %land_ref.3) | copy-start | bytes 12292
